TPU v7x, 32 devices: a whole 2x2x4 slice. The times are simulated.
32 devices in a mesh: dp: 8 (over z, y), mp: 4 (over x, core).
Axes of the slice: x: 2, y: 2, z: 4, core: 2. Of those that a mesh axis runs over, the one named last changes fastest.
Arguments:
- tokens: bfloat16 [2048, 2048], P('dp'), may hold values from -6 to 6
- out_grad: bfloat16 [2048, 2048], P('dp'), may hold values from -6 to 6
- master: float32 [2368, 3, 7168], P('dp', None, 'mp'), may hold values from -6 to 6
- moment_one: float32 [2368, 3, 7168], P('dp', None, 'mp'), may hold values from -6 to 6
- moment_two: float32 [2368, 3, 7168], P('dp', None, 'mp'), may hold values from 0.05 to 5
- old_offsets: int32 [9], replicated, may hold values from 0 to 2048, as said below
- new_offsets: int32 [9], replicated, may hold values from 0 to 2048, as said below
Outputs:
- new_master: float32 [2880, 3, 7168], P('dp', None, 'mp')
- new_moment_one: float32 [2880, 3, 7168], P('dp', None, 'mp')
- new_moment_two: float32 [2880, 3, 7168], P('dp', None, 'mp')
- layer_output: bfloat16 [2048, 2048], P('dp', 'mp')
Inputs may be any that keep to these rules, and one draw needn't show every extreme that they name: non-decreasing, old_offsets[0] = 0 and old_offsets[8] = 2048; device p holds rows old_offsets[p] to old_offsets[p + 1] - 1 in its first slots; every device holds at least one and at most 296 rows, and some device exactly 296. non-decreasing, new_offsets[0] = 0 and new_offsets[8] = 2048; exactly one device holds no rows, its index at least 2 and at most 3; every other device holds at least one and at most 360 rows, some device exactly 360; a row's device in the new layout is its device in the old layout or the next one along dp.
All inputs are finite; a program needn't handle non-finite values.
Results may differ from a plain program's by a relative error of at most 0.014.
Values may be sent and summed in bfloat16 or wider, within the bound.
A program may use at most 256 MiB of HBM per device.

v0:
```python
import functools

import jax
import jax.numpy as jnp
from jax import lax
from jax.experimental import pallas as pl
from jax.experimental.pallas import tpu as pltpu
from jax.sharding import PartitionSpec as P


FEATURE_WIDTH = 2048
FF = 7168


beta_one = 0.9
beta_two = 0.95
learn_rate = 0.01
decay_rate = 0.1
adam_eps = 1e-08
bias_one = 1.0 - 0.9**10
bias_two = 1.0 - 0.95**10


def passed_along(value, axis, by):
    peers = lax.axis_size(axis)
    pairs = [(i, i + by) for i in range(peers) if 0 <= i + by < peers]
    return lax.ppermute(value, axis, pairs)


def lookup(small_table, wanted):
    matches = wanted[..., None] == jnp.arange(small_table.shape[0], dtype=jnp.int32)
    return jnp.sum(jnp.where(matches, small_table, 0), axis=-1)


def row_layout(row_count, capacity, offsets):
    row_index = jnp.arange(row_count, dtype=jnp.int32)
    owner_index = row_index // capacity
    local_index = row_index - owner_index * capacity
    row_start = lookup(offsets, owner_index)
    in_range = local_index < lookup(offsets, owner_index + 1) - row_start
    target = jnp.clip(row_start + local_index, 0, FEATURE_WIDTH - 1)
    return (target, in_range)


def adam_step(master_rows, first_rows, second_rows, grads):
    first_new = beta_one * first_rows + (1.0 - beta_one) * grads
    second_new = beta_two * second_rows + (1.0 - beta_two) * grads * grads
    update = first_new / bias_one / (jnp.sqrt(second_new / bias_two) + adam_eps)
    master_new = master_rows - learn_rate * (update + decay_rate * master_rows)
    return (master_new, first_new, second_new)


def reshard(states, old_offsets, new_offsets, capacity_new):
    capacity_old = states.shape[0]
    from_left = passed_along(states.astype(jnp.bfloat16), "dp", 1).astype(states.dtype)
    device_index = lax.axis_index("dp")
    local_index = jnp.arange(capacity_new, dtype=jnp.int32)
    row_start = lookup(new_offsets, device_index)
    row_count = lookup(new_offsets, device_index + 1) - row_start
    in_range = local_index < row_count
    row_index = jnp.clip(row_start + local_index, 0, FEATURE_WIDTH - 1)
    owner_index = jnp.sum(
        (old_offsets[1:-1][None, :] <= row_index[:, None]).astype(jnp.int32), axis=1
    )
    slot_index = (
        (owner_index - device_index + 1) * capacity_old
        + row_index
        - lookup(old_offsets, owner_index)
    )
    neighbours = jnp.concatenate([from_left, states], axis=0)
    picked = jnp.take(neighbours, slot_index, axis=0, mode="clip")
    return jnp.where(in_range[:, None, None, None], picked, 0.0)


def train_pass(tokens, upstream, weights, layout, capacity, live_flag):
    columns = weights.shape[2]
    scale_in = FEATURE_WIDTH ** (-0.5)
    scale_hidden = FF ** (-0.5)
    contract_rows = (((0,), (0,)), ((), ()))
    shard_piece = lax.all_gather(weights, "dp", axis=0, tiled=True)
    down_rows = jnp.zeros((FEATURE_WIDTH, columns), jnp.bfloat16)
    target, in_range = row_layout(shard_piece.shape[0], capacity, layout)
    shard_piece = jnp.where(in_range[:, None, None], shard_piece, jnp.zeros_like(shard_piece))
    token_columns = jnp.take(tokens, target, axis=1, mode="clip")
    upstream_columns = jnp.take(upstream, target, axis=1, mode="clip")
    gate_sum = jnp.dot(token_columns, shard_piece[:, 0], preferred_element_type=jnp.float32)
    up_sum = jnp.dot(token_columns, shard_piece[:, 1], preferred_element_type=jnp.float32)
    back_sum = jnp.dot(upstream_columns, shard_piece[:, 2], preferred_element_type=jnp.float32)
    placed = jnp.where(in_range, target, FEATURE_WIDTH)
    down_rows = down_rows.at[placed].set(shard_piece[:, 2], mode="drop")
    gate_sum, up_sum, back_sum, down_rows = (gate_sum, up_sum, back_sum, down_rows)
    gate_act = gate_sum * scale_in
    up_act = up_sum * scale_in
    back_grad = back_sum * scale_hidden
    sigmoid_gate = jax.nn.sigmoid(gate_act)
    hidden = (gate_act * sigmoid_gate * up_act).astype(jnp.bfloat16)
    partial_value = (
        lax.dot_general(
            hidden, down_rows, (((1,), (1,)), ((), ())), preferred_element_type=jnp.float32
        )
        * scale_hidden
    )
    partial_value = jnp.where(live_flag, partial_value, 0.0)
    layer_output = lax.psum_scatter(
        partial_value.astype(jnp.bfloat16), "mp", scatter_dimension=1, tiled=True
    )
    gate_grad = (
        back_grad * up_act * sigmoid_gate * (1.0 + gate_act * (1.0 - sigmoid_gate))
    ).astype(jnp.bfloat16)
    up_grad = (back_grad * gate_act * sigmoid_gate).astype(jnp.bfloat16)
    target, in_range = row_layout(lax.axis_size("dp") * capacity, capacity, layout)
    token_columns = jnp.take(tokens, target, axis=1, mode="clip")
    upstream_columns = jnp.take(upstream, target, axis=1, mode="clip")
    gate_part = (
        lax.dot_general(token_columns, gate_grad, contract_rows, preferred_element_type=jnp.float32)
        * scale_in
    )
    up_part = (
        lax.dot_general(token_columns, up_grad, contract_rows, preferred_element_type=jnp.float32)
        * scale_in
    )
    down_part = (
        lax.dot_general(upstream_columns, hidden, contract_rows, preferred_element_type=jnp.float32)
        * scale_hidden
    )
    stacked = jnp.stack([gate_part, up_part, down_part], axis=1)
    grads = lax.psum_scatter(
        jnp.where(in_range[:, None, None], stacked, 0.0).astype(jnp.bfloat16),
        "dp",
        scatter_dimension=0,
        tiled=True,
    ).astype(jnp.float32)
    return (grads, layer_output)


def body(tokens, out_grad, master, moment_one, moment_two, old_offsets, new_offsets):
    devices = lax.axis_size("dp")
    shard_rows = FEATURE_WIDTH // devices
    jitter_rows = shard_rows // (2 * (devices - 1)) + 2
    capacity_new = shard_rows + shard_rows // 4 + 2 * jitter_rows
    device_index = lax.axis_index("dp")
    live_flag = lookup(new_offsets, device_index + 1) != lookup(new_offsets, device_index)
    upstream = jnp.where(live_flag, out_grad, jnp.zeros_like(out_grad))
    states = jnp.stack([master, moment_one, moment_two], axis=1)
    weights = states[:, 0].astype(jnp.bfloat16)
    grads, layer_output = train_pass(
        tokens, upstream, weights, old_offsets, states.shape[0], live_flag
    )
    updated = jnp.stack(adam_step(states[:, 0], states[:, 1], states[:, 2], grads), axis=1)
    updated = reshard(updated, old_offsets, new_offsets, capacity_new)
    return (updated[:, 0], updated[:, 1], updated[:, 2], layer_output)


ANY = pl.BlockSpec(memory_space=pl.ANY)
WHOLE = pl.BlockSpec(memory_space=pltpu.VMEM)


def remote(source, target, send, recv, **where):
    return pltpu.make_async_remote_copy(
        src_ref=source,
        dst_ref=target,
        send_sem=send,
        recv_sem=recv,
        device_id=where,
        device_id_type=pl.DeviceIdType.MESH,
    )


def greet(peers):
    me = lax.axis_index("dp")
    unit = lax.axis_index("mp")
    barrier = pltpu.get_barrier_semaphore()
    for off in range(1, peers):
        pl.semaphore_signal(
            barrier,
            inc=1,
            device_id={"dp": (me + off) % peers},
            device_id_type=pl.DeviceIdType.MESH,
        )
    for other in (other_core(unit), other_chip(unit)):
        pl.semaphore_signal(
            barrier, inc=1, device_id={"mp": other}, device_id_type=pl.DeviceIdType.MESH
        )
    pl.semaphore_wait(barrier, peers + 1)


IDLE = 0


def first_column(dp, width):
    return pl.multiple_of(jnp.maximum(dp - 1, 0) * width, 128)


def other_core(unit):
    return unit + 1 - 2 * (unit % 2)


def other_chip(unit):
    return (unit + 2) % 4


def spread_kernel(peers, width, weights, tokens, upstream, far, blocks, all_tokens, all_upstream,
                  crossed_far, w_send, w_recv, z_send, z_recv, y_send, y_recv, x_send, x_recv,
                  c_send, c_recv, f_send, f_recv, own_sem):
    me = lax.axis_index("dp")
    unit = lax.axis_index("mp")
    planes = peers // 2
    z, y = me // 2, me % 2
    core, chip = other_core(unit), other_chip(unit)
    kinds = weights.shape[0]
    group = tokens.shape[0]
    piece = group // 4
    sources = (tokens, upstream)
    wholes = (all_tokens, all_upstream)
    beside = z * 2 + 1 - y

    def owner(shift, same):
        return (z + shift) * 2 + (y if same else 1 - y)

    def quarter(which, dp, unit):
        return wholes[which].at[pl.ds(pl.multiple_of(dp * group + unit * piece, piece), piece)]

    def mine(which):
        return sources[which].at[pl.ds(pl.multiple_of(unit * piece, piece), piece)]

    def along_y(which):
        return remote(
            mine(which), quarter(which, me, unit), y_send.at[which], y_recv.at[which], dp=beside
        )

    def along_y_in(which):
        here = quarter(which, beside, unit)
        return remote(here, here, y_send.at[which], y_recv.at[which], dp=beside)

    def z_slot(dz, step):
        return step + (planes if dz < 0 else 0)

    def along_z(which, dz, step, same):
        there = quarter(which, owner(-dz * step, same), unit)
        slot = z_slot(dz, step)
        return remote(
            mine(which) if step == 0 and same else there, there,
            z_send.at[which, slot, same], z_recv.at[which, slot, same], dp=(z + dz) * 2 + y,
        )

    def along_z_in(which, dz, step, same):
        here = quarter(which, owner(-dz * step, same), unit)
        slot = z_slot(dz, step - 1)
        return remote(
            here, here, z_send.at[which, slot, same], z_recv.at[which, slot, same],
            dp=(z - dz) * 2 + y,
        )

    def slot_of(shift, same):
        return 2 * (shift + planes - 1) + same

    def along_x(which, shift, same):
        here = quarter(which, owner(shift, same), unit)
        slot = slot_of(shift, same)
        return remote(here, here, x_send.at[which, slot], x_recv.at[which, slot], mp=chip)

    def along_x_in(which, shift, same):
        here = quarter(which, owner(shift, same), chip)
        slot = slot_of(shift, same)
        return remote(here, here, x_send.at[which, slot], x_recv.at[which, slot], mp=chip)

    def to_core(which, shift, same, crossed):
        here = quarter(which, owner(shift, same), chip if crossed else unit)
        slot = slot_of(shift, same)
        return remote(
            here, here, c_send.at[which, slot, crossed], c_recv.at[which, slot, crossed], mp=core
        )

    def to_core_in(which, shift, same, crossed):
        here = quarter(which, owner(shift, same), other_chip(core) if crossed else core)
        slot = slot_of(shift, same)
        return remote(
            here, here, c_send.at[which, slot, crossed], c_recv.at[which, slot, crossed], mp=core
        )

    def weight(off, kind):
        peer = (me + off) % peers
        return remote(
            weights.at[kind, :, pl.ds(first_column(peer, width), width)],
            blocks.at[me, :, pl.ds(kind * width, width)],
            w_send.at[off - 1, kind], w_recv.at[off - 1, kind], dp=peer,
        )

    def weight_in(off, kind):
        peer = (me + peers - off) % peers
        here = blocks.at[peer, :, pl.ds(kind * width, width)]
        return remote(here, here, w_send.at[off - 1, kind], w_recv.at[off - 1, kind], dp=peer)

    def weights_out(offs):
        for off in offs:
            @pl.when((me + off) % peers != IDLE)
            def _():
                for kind in range(kinds):
                    weight(off, kind).start()

    def far_rows(which, kind):
        return remote(
            far.at[which, kind], crossed_far.at[which, kind],
            f_send.at[which, kind], f_recv.at[which, kind], dp=beside,
        )

    up, down = z < planes - 1, z > 0

    def each_z(act):
        for dz, further in ((1, up), (-1, down)):
            @pl.when(further)
            def _():
                act(dz)

    def each_z_in(step, act):
        for dz, further in ((1, up), (-1, down)):
            there = (z >= step) if dz > 0 else (z + step < planes)
            act(dz, there, there & further)

    greet(peers)
    for which in range(2):
        along_y(which).start()
        each_z(lambda dz: along_z(which, dz, 0, 1).start())

    own_rows = [
        pltpu.make_async_copy(
            sources[which],
            wholes[which].at[pl.ds(pl.multiple_of(me * group, group), group)],
            own_sem.at[which],
        )
        for which in range(2)
    ]
    own_rows += [
        pltpu.make_async_copy(
            weights.at[kind, :, pl.ds(first_column(me, width), width)],
            blocks.at[me, :, pl.ds(kind * width, width)],
            own_sem.at[2 + kind],
        )
        for kind in range(kinds)
    ]
    for copy in own_rows:
        copy.start()

    offsets = sorted(range(1, peers), key=lambda off: abs(2 * off - peers))
    share = -(-len(offsets) // planes)
    weights_out(offsets[:share])

    def share_on(which, shift, same):
        along_x(which, shift, same).start()
        to_core(which, shift, same, 0).start()

    for which in range(2):
        along_y_in(which).wait_recv()
        each_z(lambda dz: along_z(which, dz, 0, 0).start())
        share_on(which, 0, 0)

    for step in range(1, planes):
        for which in range(2):
            for same in (1, 0):
                def receive(dz, there, goes_on):
                    @pl.when(there)
                    def _():
                        along_z_in(which, dz, step, same).wait_recv()

                    @pl.when(goes_on)
                    def _():
                        along_z(which, dz, step, same).start()

                    @pl.when(there)
                    def _():
                        share_on(which, -dz * step, same)

                each_z_in(step, receive)
        weights_out(offsets[share * step : share * (step + 1)])
        if step == 1:
            for which in range(far.shape[0]):
                for kind in range(kinds):
                    far_rows(which, kind).start()

    def everywhere(act):
        for step in range(planes):
            for which in range(2):
                for dz in (1, -1) if step else (1,):
                    there = (z >= step) if dz > 0 else (z + step < planes)

                    @pl.when(there)
                    def _():
                        for same in (1, 0) if step else (0,):
                            act(which, -dz * step, same)

    def cross(which, shift, same):
        along_x_in(which, shift, same).wait_recv()
        to_core(which, shift, same, 1).start()

    def finish(which, shift, same):
        for crossed in range(2):
            to_core_in(which, shift, same, crossed).wait_recv()
        along_x(which, shift, same).wait_send()
        for crossed in range(2):
            to_core(which, shift, same, crossed).wait_send()

    everywhere(cross)
    everywhere(finish)

    for which in range(2):
        along_y(which).wait_send()
        for same in (1, 0):
            each_z(lambda dz: along_z(which, dz, 0, same).wait_send())
            for step in range(1, planes):
                def sent(dz, there, goes_on):
                    @pl.when(goes_on)
                    def _():
                        along_z(which, dz, step, same).wait_send()

                each_z_in(step, sent)

    for off in range(1, peers):
        @pl.when((me + off) % peers != IDLE)
        def _():
            for kind in range(kinds):
                weight(off, kind).wait_send()

    @pl.when(me != IDLE)
    def _():
        for off in range(1, peers):
            for kind in range(kinds):
                weight_in(off, kind).wait_recv()

    for which in range(far.shape[0]):
        for kind in range(kinds):
            far_rows(which, kind).wait()
    for copy in own_rows:
        copy.wait()


def spread(weights, tokens, upstream, far, peers, width):
    kinds, rows, _ = weights.shape
    group, features = tokens.shape
    planes = peers // 2
    dma = pltpu.SemaphoreType.DMA
    return pl.pallas_call(
        functools.partial(spread_kernel, peers, width),
        out_shape=(
            jax.ShapeDtypeStruct((peers, rows, kinds * width), weights.dtype),
            jax.ShapeDtypeStruct((peers * group, features), tokens.dtype),
            jax.ShapeDtypeStruct((peers * group, features), tokens.dtype),
            jax.ShapeDtypeStruct(far.shape, far.dtype),
        ),
        in_specs=[WHOLE] * 3 + [ANY],
        out_specs=[ANY] * 4,
        scratch_shapes=[
            dma((peers - 1, kinds)), dma((peers - 1, kinds)),
            dma((2, 2 * planes, 2)), dma((2, 2 * planes, 2)),
            dma((2,)), dma((2,)),
            dma((2, 4 * planes)), dma((2, 4 * planes)),
            dma((2, 4 * planes, 2)), dma((2, 4 * planes, 2)),
            dma(far.shape[:2]), dma(far.shape[:2]),
            dma((2 + kinds,)),
        ],
        compiler_params=pltpu.CompilerParams(
            collective_id=0, has_side_effects=True, vmem_limit_bytes=24 << 20
        ),
        name="spread",
    )(weights, tokens, upstream, far)


def swap_kernel(peers, width, shares, *refs):
    if shares:
        packed, parts, arrived, gathered, send, recv, own_sem, p_send, p_recv, p_own = refs
    else:
        packed, arrived, send, recv, own_sem = refs
    me = lax.axis_index("dp")
    kinds = arrived.shape[0]
    barrier = pltpu.get_barrier_semaphore()
    for off in range(1, peers):
        pl.semaphore_signal(
            barrier,
            inc=1,
            device_id={"dp": (me + off) % peers},
            device_id_type=pl.DeviceIdType.MESH,
        )
    pl.semaphore_wait(barrier, peers - 1)

    def place(dp, kind):
        return arrived.at[kind, :, pl.ds(first_column(dp, width), width)]

    def out(off, kind):
        peer = (me + off) % peers
        return remote(
            packed.at[peer, :, pl.ds(kind * width, width)], place(me, kind),
            send.at[off - 1, kind], recv.at[off - 1, kind], dp=peer,
        )

    def into(off, kind):
        peer = (me + peers - off) % peers
        here = place(peer, kind)
        return remote(here, here, send.at[off - 1, kind], recv.at[off - 1, kind], dp=peer)

    def part(off):
        peer = (me + off) % peers
        return remote(
            parts.at[peer], gathered.at[me], p_send.at[off - 1], p_recv.at[off - 1], dp=peer
        )

    def part_in(off):
        peer = (me + peers - off) % peers
        here = gathered.at[peer]
        return remote(here, here, p_send.at[off - 1], p_recv.at[off - 1], dp=peer)

    own = [
        pltpu.make_async_copy(
            packed.at[me, :, pl.ds(kind * width, width)], place(me, kind), own_sem.at[kind]
        )
        for kind in range(kinds)
    ]
    offsets = sorted(range(1, peers), key=lambda off: abs(2 * off - peers))
    if shares:
        own_part = pltpu.make_async_copy(parts.at[me], gathered.at[me], p_own)
        for off in offsets:
            part(off).start()
        own_part.start()

    @pl.when(me != IDLE)
    def _():
        for off in offsets:
            for kind in range(kinds):
                out(off, kind).start()
        for copy in own:
            copy.start()

    if shares:
        for off in offsets:
            part_in(off).wait_recv()
            part(off).wait_send()
        own_part.wait()
    for off in range(1, peers):
        @pl.when((me + peers - off) % peers != IDLE)
        def _():
            for kind in range(kinds):
                into(off, kind).wait_recv()

    @pl.when(me != IDLE)
    def _():
        for off in range(1, peers):
            for kind in range(kinds):
                out(off, kind).wait_send()
        for copy in own:
            copy.wait()


def swap(packed, kinds, columns, shares=None):
    peers, rows, across = packed.shape
    dma = pltpu.SemaphoreType.DMA
    out_shape = [jax.ShapeDtypeStruct((kinds, rows, columns), packed.dtype)]
    scratch = [dma((peers - 1, kinds)), dma((peers - 1, kinds)), dma((kinds,))]
    operands = [packed]
    if shares is not None:
        operands.append(shares)
        out_shape.append(jax.ShapeDtypeStruct(shares.shape, shares.dtype))
        scratch += [dma((peers - 1,)), dma((peers - 1,)), dma]
    return pl.pallas_call(
        functools.partial(swap_kernel, peers, across // kinds, shares is not None),
        out_shape=out_shape,
        in_specs=[WHOLE] * len(operands),
        out_specs=[ANY] * len(out_shape),
        scratch_shapes=scratch,
        compiler_params=pltpu.CompilerParams(
            collective_id=1 + len(out_shape), has_side_effects=True, vmem_limit_bytes=16 << 20
        ),
        name="swap",
    )(*operands)


STEP_ROWS = 40


def shifted(ref, which, start):
    wide = STEP_ROWS + 8
    down = start % 8
    rows = ref[which, pl.ds(pl.multiple_of(start - down, 8), wide), :]
    rows = pltpu.roll(rows.reshape(wide // 8, 8, rows.shape[1]), 8 - down, 1)
    inside = lax.broadcasted_iota(jnp.int32, rows[1:].shape, 1) < 8 - down
    return jnp.where(inside, rows[:-1], rows[1:]).reshape(STEP_ROWS, rows.shape[2])


def adam_kernel(numbers, *refs):
    owns, near, straight, relayed, grads, last_grads = refs[:3], *refs[3:8]
    outs, from_own, from_left = refs[8:11], refs[11], refs[12]
    arrived, left_skip, count, odd = numbers[0], numbers[1], numbers[2], numbers[3]
    capacity_old = owns[0].shape[1]
    capacity_new = outs[0].shape[1]
    half = near.shape[2]
    for which in range(3):
        from_own[which, pl.ds(capacity_new, capacity_old), :] = owns[which][0]
        from_left[which, pl.ds(0, half), :] = near[which, 0].astype(jnp.float32)
        far = pl.ds(half, capacity_old - half)
        value = jnp.where(odd > 0, straight[which, 0], relayed[which, 0])
        from_left[which, far, :] = value.astype(jnp.float32)
    kinds = pl.num_programs(0)
    is_last = pl.program_id(0) == kinds - 1

    def some_rows(step, carry):
        first = pl.multiple_of(step * STEP_ROWS, 8)
        slot = first + lax.broadcasted_iota(jnp.int32, (STEP_ROWS, outs[0].shape[2]), 0)
        rows = [
            jnp.where(
                slot < arrived,
                shifted(from_left, which, first + left_skip),
                shifted(from_own, which, first + capacity_new - arrived),
            )
            for which in range(3)
        ]
        here = pl.ds(first, STEP_ROWS)
        grad = jnp.where(is_last, last_grads[0, here, :], grads[0, here, :]).astype(jnp.float32)
        updated = adam_step(rows[0], rows[1], rows[2], grad)
        for which in range(3):
            outs[which][0, here, :] = jnp.where(slot < count, updated[which], 0.0)
        return carry

    lax.fori_loop(0, capacity_new // STEP_ROWS, some_rows, 0)


def adam(states, moved, grads, last_grads, numbers):
    kinds, capacity_old, columns = states[0].shape
    capacity_new = grads.shape[1]
    width = columns // 2 if columns % 256 == 0 else columns

    def block(rows):
        return pl.BlockSpec((1, rows, width), lambda kind, part, _: (kind, 0, part))

    def stacked(rows):
        return pl.BlockSpec((3, 1, rows, width), lambda kind, part, _: (0, kind, 0, part))

    first_grads = pl.BlockSpec(
        (1, capacity_new, width), lambda kind, part, _: (jnp.minimum(kind, kinds - 2), 0, part)
    )
    third_grads = pl.BlockSpec((1, capacity_new, width), lambda kind, part, _: (0, 0, part))
    return pl.pallas_call(
        adam_kernel,
        out_shape=[jax.ShapeDtypeStruct((kinds, capacity_new, columns), jnp.float32)] * 3,
        grid_spec=pltpu.PrefetchScalarGridSpec(
            num_scalar_prefetch=1,
            grid=(kinds, columns // width),
            in_specs=[block(capacity_old)] * 3
            + [stacked(value.shape[2]) for value in moved]
            + [first_grads, third_grads],
            out_specs=[block(capacity_new)] * 3,
            scratch_shapes=[
                pltpu.VMEM((3, 2 * capacity_new + 8, width), jnp.float32),
                pltpu.VMEM((3, capacity_new + capacity_old + 8, width), jnp.float32),
            ],
        ),
        compiler_params=pltpu.CompilerParams(vmem_limit_bytes=60 << 20),
        name="adam",
    )(numbers, *states, *moved, grads, last_grads)


def cast_kernel(*refs):
    owns, near, far, weights = refs[:3], refs[3], refs[4], refs[5]
    half = near.shape[2]
    for which in range(3):
        near[which, 0] = owns[which][0, :half, :].astype(near.dtype)
        far[which, 0] = owns[which][0, half:, :].astype(far.dtype)
    weights[0] = owns[0][0].astype(weights.dtype)


def cast(states):
    kinds, rows, columns = states[0].shape
    width = columns // 2 if columns % 256 == 0 else columns
    half = (rows + 15) // 16 * 8
    stacked = [(3, kinds, half, columns), (3, kinds, rows - half, columns)]
    whole = pl.BlockSpec((1, rows, width), lambda kind, part: (kind, 0, part))
    return pl.pallas_call(
        cast_kernel,
        out_shape=[jax.ShapeDtypeStruct(shape, jnp.bfloat16) for shape in stacked]
        + [jax.ShapeDtypeStruct(states[0].shape, jnp.bfloat16)],
        grid=(kinds, columns // width),
        in_specs=[whole] * 3,
        out_specs=[
            pl.BlockSpec((3, 1, shape[2], width), lambda kind, part: (0, kind, 0, part))
            for shape in stacked
        ]
        + [whole],
        compiler_params=pltpu.CompilerParams(vmem_limit_bytes=32 << 20),
        name="cast",
    )(*states)


def lane_split(columns, peers):
    return -(-columns // (peers * 128)) * 128


def product(left, right, left_dim, right_dim):
    return lax.dot_general(
        left,
        right,
        (((left_dim,), (right_dim,)), ((), ())),
        preferred_element_type=jnp.float32,
    )


def token_pass(tokens, upstream, weights, far, old_offsets, new_offsets, capacity_new):
    peers = lax.axis_size("dp")
    feature_peers = lax.axis_size("mp")
    kinds, capacity_old, columns = weights.shape
    width = lane_split(columns, peers)
    features = tokens.shape[1]
    scale_in = features ** (-0.5)
    scale_hidden = (columns * feature_peers) ** (-0.5)
    busy = lax.axis_index("dp") != IDLE

    blocks, all_tokens, all_upstream, straight = spread(
        weights, tokens, upstream, far, peers, width
    )
    blocks = blocks.reshape(peers * capacity_old, kinds * width)
    target, in_range = row_layout(peers * capacity_old, capacity_old, old_offsets)
    target = jnp.where(in_range, target, features)
    wanted = jnp.arange(features, dtype=jnp.int32)[:, None] == target[None, :]
    rows = product(wanted.astype(jnp.bfloat16), blocks, 1, 0)
    rows = jnp.where(busy, rows, 0.0).astype(jnp.bfloat16)
    rows = lax.optimization_barrier(rows)
    rows = [rows[:, kind * width : (kind + 1) * width] for kind in range(kinds)]

    gate_act = product(all_tokens, rows[0], 1, 0) * scale_in
    up_act = product(all_tokens, rows[1], 1, 0) * scale_in
    back_grad = product(all_upstream, rows[2], 1, 0) * scale_hidden
    sigmoid_gate = jax.nn.sigmoid(gate_act)
    hidden = (gate_act * sigmoid_gate * up_act).astype(jnp.bfloat16)
    gate_grad = (
        back_grad * up_act * sigmoid_gate * (1.0 + gate_act * (1.0 - sigmoid_gate))
    ).astype(jnp.bfloat16)
    up_grad = (back_grad * gate_act * sigmoid_gate).astype(jnp.bfloat16)

    partial_value = (product(hidden, rows[2], 1, 1) * scale_hidden).astype(jnp.bfloat16)
    partial_value = lax.psum_scatter(partial_value, "mp", scatter_dimension=1, tiled=True)
    shares = partial_value.reshape(peers, -1, partial_value.shape[1])

    target, in_range = row_layout(peers * capacity_new, capacity_new, new_offsets)
    target = jnp.where(in_range, target, features)
    wanted = target[:, None] == jnp.arange(features, dtype=jnp.int32)[None, :]
    wanted = wanted.astype(jnp.bfloat16)

    def packed(value):
        value = lax.optimization_barrier(value)
        value = product(wanted, value, 1, 0).astype(jnp.bfloat16)
        return value.reshape(peers, capacity_new, -1)

    grads = [
        (product(all_tokens, gate_grad, 0, 0) * scale_in).astype(jnp.bfloat16),
        (product(all_tokens, up_grad, 0, 0) * scale_in).astype(jnp.bfloat16),
    ]
    last_grads = (product(all_upstream, hidden, 0, 0) * scale_hidden).astype(jnp.bfloat16)
    first_packed = packed(jnp.concatenate(grads, axis=1))
    last_packed = packed(last_grads)
    (grads,) = swap(first_packed, kinds - 1, columns)
    last_grads, shares = swap(last_packed, 1, columns, shares)
    layer_output = jnp.sum(shares.astype(jnp.float32), axis=0).astype(jnp.bfloat16)
    return grads, last_grads, layer_output, straight


def token_body(*arguments):
    return token_step(*arguments)


def token_step(tokens, out_grad, master, moment_one, moment_two, old_offsets, new_offsets):
    devices = lax.axis_size("dp")
    capacity_old = master.shape[0]
    capacity_new = new_capacity(tokens.shape[1], devices)
    device_index = lax.axis_index("dp")
    new_start = lookup(new_offsets, device_index)
    new_end = lookup(new_offsets, device_index + 1)
    old_start = lookup(old_offsets, device_index)
    left_start = lookup(old_offsets, jnp.maximum(device_index - 1, 0))
    live_flag = new_end != new_start
    upstream = jnp.where(live_flag, out_grad, jnp.zeros_like(out_grad))

    states = [value.transpose(1, 0, 2) for value in (master, moment_one, moment_two)]
    near, far, weights = cast(states)
    near = lax.ppermute(near, "dp", [(i, i + 1) for i in range(devices - 1)])
    grads, last_grads, layer_output, straight = token_pass(
        tokens, upstream, weights, far, old_offsets, new_offsets, capacity_new
    )
    relayed = lax.ppermute(straight, "dp", [(i, i + 2) for i in range(0, devices - 2, 2)])
    moved = (near, straight, relayed)
    arrived = jnp.clip(old_start - new_start, 0, capacity_new)
    left_skip = jnp.clip(new_start - left_start, 0, capacity_old)
    numbers = jnp.stack([arrived, left_skip, new_end - new_start, device_index % 2])
    updated = adam(states, moved, grads, last_grads, numbers)
    updated = [value.transpose(1, 0, 2) for value in updated]
    layer_output = jnp.where(live_flag, layer_output, jnp.zeros_like(layer_output))
    return (updated[0], updated[1], updated[2], layer_output)


def new_capacity(features, devices):
    shard_rows = features // devices
    jitter_rows = shard_rows // (2 * (devices - 1)) + 2
    return shard_rows + shard_rows // 4 + 2 * jitter_rows


def any_body(tokens, out_grad, master, *others):
    devices = lax.axis_size("dp")
    columns = master.shape[2]
    moved_tokens = 3 * tokens.shape[0] * devices
    moved_rows = 2 * master.shape[1] * columns
    whole = (
        devices % 2 == 0
        and lax.axis_size("mp") == 4
        and tokens.shape[0] % 64 == 0
        and columns == (devices - 1) * lane_split(columns, devices)
        and new_capacity(tokens.shape[1], devices) % STEP_ROWS == 0
    )
    chosen = token_body if whole and moved_tokens <= moved_rows else body
    return chosen(tokens, out_grad, master, *others)


def solution(mesh):
    placed = (
        P("dp", None),
        P("dp", None),
        P("dp", None, "mp"),
        P("dp", None, "mp"),
        P("dp", None, "mp"),
        P(),
        P(),
    )
    return jax.shard_map(
        any_body,
        mesh=mesh,
        in_specs=placed,
        out_specs=(P("dp", None, "mp"), P("dp", None, "mp"), P("dp", None, "mp"), P("dp", "mp")),
        check_vma=False,
    )
```

profile of v0, /device:TPU:9, one launch (start us, length us, event | category | flops | bytes accessed | tf_op | source)
XLA Modules:
  0.0 543.9 jit_solution(5843603462080484320)
XLA Ops:
  7.2 1.4 fusion.23
  10.9 2.8 copy-done
  13.7 7.1 %cast.1 = (bf16[3,3,152,1792]{3,2,1,0:T(8,128)(2,1)S(1)}, bf16[3,3,144,1792]{3,2,1,0:T(8,128)(2,1)S(1)}, bf16[3,296,1792]{2,1,0:T(8,128)(2,1)S(1)}) custom-call(f32[3,296,1792]{2,1,0:T(8,128)S(1)} %bitcast.26, f32[3,296,1792]{2,1,0:T(8,128)} %bitcast.33, f32[3,296,1792]{2,1,0:T(8,128)} %bitcast.35), custom_call_target="tpu_custom_call" | custom-call | tf_op jit(solution)/shard_map/cast/pallas_call | solution.py:673
  20.8 2.2 copy-done.8
  23.0 180.0 %spread.1 = (bf16[8,296,768]{2,1,0:T(8,128)(2,1)S(1)}, bf16[2048,2048]{1,0:T(8,128)(2,1)S(1)}, bf16[2048,2048]{1,0:T(8,128)(2,1)}, bf16[3,3,144,1792]{3,2,1,0:T(8,128)(2,1)S(1)}) custom-call(bf16[3,296,1792]{2,1,0:T(8,128)(2,1)S(1)} %get-tuple-element.17.weights, bf16[256,2048]{1,0:T(8,128)(2,1)S(1)} %copy-done.6, ...), custom_call_target="tpu_custom_call" | custom-call | tf_op jit(solution)/shard_map/spread/pallas_call | solution.py:441
  203.0 9.3 %select_convert_fusion = bf16[2048,768]{1,0:T(8,128)(2,1)S(1)} fusion(bf16[2368,768]{1,0:T(8,128)(2,1)S(1)} %bitcast.32, s32[2368]{0:T(1024)S(1)} %clamp_select_fusion, pred[]{:T(512)S(6)} %ne.116), kind=kOutput, calls=%fused_computation.9 | convolution fusion | flops 7457079296 | bytes 6792449 | tf_op jit(solution)/shard_map/dot_general | solution.py:694
  212.4 2.4 convolution_multiply_fusion.3
  214.9 4.2 multiply_convert_fusion.1
  220.1 5.6 %multiply_convert_fusion = bf16[2048,2048]{1,0:T(8,128)(2,1)} fusion(bf16[2048,256]{1,0:T(8,128)(2,1)S(1)} %get-tuple-element.36, bf16[2048,768]{1,0:T(8,128)(2,1)S(1)} %select_convert_fusion), kind=kOutput, calls=%fused_computation.5 | convolution fusion | flops 2155872256 | bytes 10485760 | tf_op jit(solution)/shard_map/dot_general | solution.py:694
  225.7 4.1 collective-permute-start
  229.8 18.0 %collective-permute-start.1 = (bf16[3,3,144,1792]{3,2,1,0:T(8,128)(2,1)}, bf16[3,3,144,1792]{3,2,1,0:T(8,128)(2,1)}, u32[]{:S(2)}, u32[]{:S(2)}) collective-permute-start(bf16[3,3,144,1792]{3,2,1,0:T(8,128)(2,1)} %copy-done.2), channel_id=1, source_target_pairs={{0,8},{8,16},{16,24},{1,9},{9,17},{17,25},{2,10},{10,18},{18,26},{... | collective-permute-start | bytes 13934600 | tf_op jit(solution)/shard_map/ppermute | solution.py:783
  247.9 6.7 %convolution_multiply_fusion.5 = f32[2048,256]{1,0:T(8,128)S(1)} fusion(bf16[2048,2048]{1,0:T(8,128)(2,1)} %get-tuple-element.21, bf16[2048,768]{1,0:T(8,128)(2,1)S(1)} %select_convert_fusion), kind=kOutput, calls=%fused_computation.17 | convolution fusion | flops 2148007936 | bytes 11534336 | tf_op jit(solution)/shard_map/dot_general | solution.py:694
  254.6 8.4 %fusion.8 = bf16[2048,256]{1,0:T(8,128)(2,1)S(1)} fusion(bf16[2048,2048]{1,0:T(8,128)(2,1)} %copy-done.7, f32[2048,256]{1,0:T(8,128)S(1)} %copy-done.13, f32[2048,256]{1,0:T(8,128)S(1)} %convolution_multiply_fusion.5, f32[2048,256]{1,0:T(8,128)S(1)} %copy-done.14), kind=kOutput, calls=%fused_computation.18 | convolution fusion | flops 2153775104 | bytes 15728640 | tf_op jit(solution)/shard_map/dot_general | solution.py:694
  263.1 2.9 fusion.9
  270.2 5.9 %fusion.10 = bf16[2048,256]{1,0:T(8,128)(2,1)S(1)} fusion(bf16[2048,2048]{1,0:T(8,128)(2,1)} %get-tuple-element.21, bf16[2048,256]{1,0:T(8,128)(2,1)S(1)} %copy-done.11), kind=kOutput, calls=%fused_computation.20 | convolution fusion | flops 2148532224 | bytes 10485760 | tf_op jit(solution)/shard_map/dot_general | solution.py:694
  276.3 7.5 %fusion.6 = bf16[2880,512]{1,0:T(8,128)(2,1)S(1)} fusion(bf16[2048,512]{1,0:T(8,128)(2,1)S(1)} %pad_maximum_fusion, s32[2880]{0:T(1024)S(1)} %clamp_select_fusion.1), kind=kOutput, calls=%fused_computation.10 | convolution fusion | flops 6047170560 | bytes 5057792 | tf_op jit(solution)/shard_map/dot_general | solution.py:694
  283.8 99.7 %swap.2.refs_6_ = bf16[2,360,1792]{2,1,0:T(8,128)(2,1)S(1)} custom-call(bf16[8,360,512]{2,1,0:T(8,128)(2,1)S(1)} %bitcast.27), custom_call_target="tpu_custom_call" | custom-call | tf_op jit(solution)/shard_map/swap/pallas_call | solution.py:561
  383.5 1.5 copy-done.1
  385.7 5.4 fusion.7
  391.1 1.6 copy-done.3
  392.7 1.4 copy-done.4
  394.1 113.2 %swap.3 = (bf16[1,360,1792]{2,1,0:T(8,128)(2,1)S(1)}, bf16[8,256,512]{2,1,0:T(8,128)(2,1)S(1)}) custom-call(bf16[8,360,256]{2,1,0:T(8,128)(2,1)S(1)} %bitcast.29, bf16[8,256,512]{2,1,0:T(8,128)(2,1)S(1)} %bitcast.28), custom_call_target="tpu_custom_call" | custom-call | tf_op jit(solution)/shard_map/swap/pallas_call | solution.py:561
  507.2 1.0 copy-done.5
  509.4 27.6 %adam.1 = (f32[3,360,1792]{2,1,0:T(8,128)}, f32[3,360,1792]{2,1,0:T(8,128)}, f32[3,360,1792]{2,1,0:T(8,128)}) custom-call(s32[4]{0:T(128)} %pad_add_fusion.numbers, f32[3,296,1792]{2,1,0:T(8,128)} %bitcast.25, f32[3,296,1792]{2,1,0:T(8,128)} %bitcast.34, f32[3,296,1792]{2,1,0:T(8,128)} %bitcast.36, bf16[3,3,152,1792]{3,2,1,0:T(8,128)(2,1)} %collective-permute-done.refs_3_, ...), custom_call_target="tpu_custom_call" | custom-call | tf_op jit(solution)/shard_map/adam/pallas_call | solution.py:638
  (45 shorter events, 4.1 us)
Async XLA Ops:
  7.2 383.9 %reduce-scatter.2.cloned.1.call-start = ((), (), s32[]{:S(2)}) async-start(), calls=%async_computation.1 | async-start | bytes 10485760 | tf_op jit(solution)/shard_map/reduce_scatter | solution.py:735
  10.9 2.8 copy-start
  13.7 9.4 %copy-start.6 = (bf16[256,2048]{1,0:T(8,128)(2,1)S(1)}, bf16[256,2048]{1,0:T(8,128)(2,1)}, u32[]{:S(2)}) copy-start(bf16[256,2048]{1,0:T(8,128)(2,1)} %tokens.1) | copy-start | bytes 3145732
  20.8 2.2 copy-start.8
  203.0 9.4 %copy-start.2 = (bf16[3,3,144,1792]{3,2,1,0:T(8,128)(2,1)}, bf16[3,3,144,1792]{3,2,1,0:T(8,128)(2,1)S(1)}, u32[]{:S(2)}) copy-start(bf16[3,3,144,1792]{3,2,1,0:T(8,128)(2,1)S(1)} %get-tuple-element.19.refs_4_) | copy-start | bytes 13934596
  203.0 11.8 %copy-start.7 = (bf16[2048,2048]{1,0:T(8,128)(2,1)}, bf16[2048,2048]{1,0:T(8,128)(2,1)S(1)}, u32[]{:S(2)}) copy-start(bf16[2048,2048]{1,0:T(8,128)(2,1)S(1)} %get-tuple-element.20) | copy-start | bytes 25165828
  214.8 4.2 copy-start.12
  219.1 1.0 copy-start.10
  225.7 283.7 %collective-permute-start = (bf16[3,3,152,1792]{3,2,1,0:T(8,128)(2,1)}, bf16[3,3,152,1792]{3,2,1,0:T(8,128)(2,1)}, u32[]{:S(2)}, u32[]{:S(2)}) collective-permute-start(bf16[3,3,152,1792]{3,2,1,0:T(8,128)(2,1)} %copy-done.8), channel_id=1, source_target_pairs={{0,4},{4,8},{8,12},{12,16},{16,20},{20,24},{24,28},{1,5},{5,9},{9,... | collective-permute-start | bytes 14708744 | tf_op jit(solution)/shard_map/ppermute | solution.py:779
  229.8 279.6 %collective-permute-start.1 = (bf16[3,3,144,1792]{3,2,1,0:T(8,128)(2,1)}, bf16[3,3,144,1792]{3,2,1,0:T(8,128)(2,1)}, u32[]{:S(2)}, u32[]{:S(2)}) collective-permute-start(bf16[3,3,144,1792]{3,2,1,0:T(8,128)(2,1)} %copy-done.2), channel_id=1, source_target_pairs={{0,8},{8,16},{16,24},{1,9},{9,17},{17,25},{2,10},{10,18},{18,26},{... | collective-permute-start | bytes 13934600 | tf_op jit(solution)/shard_map/ppermute | solution.py:783
  247.8 6.7 %copy-start.13 = (f32[2048,256]{1,0:T(8,128)S(1)}, f32[2048,256]{1,0:T(8,128)}, u32[]{:S(2)}) copy-start(f32[2048,256]{1,0:T(8,128)} %copy-done.12) | copy-start | bytes 6291460
  247.8 6.7 %copy-start.14 = (f32[2048,256]{1,0:T(8,128)S(1)}, f32[2048,256]{1,0:T(8,128)}, u32[]{:S(2)}) copy-start(f32[2048,256]{1,0:T(8,128)} %get-tuple-element.37) | copy-start | bytes 6291460
  247.9 15.2 %slice-start = ((s8[8388608]{0:T(1024)(128)(4,1)}), s8[4194304]{0:T(1024)(128)(4,1)S(1)}, s32[]{:S(2)}) async-start(s8[8388608]{0:T(1024)(128)(4,1)} %bitcast.30), calls=%async_computation.2 | async-start | bytes 8388608
  254.6 8.5 %slice-start.1 = ((s8[8388608]{0:T(1024)(128)(4,1)}), s8[4194304]{0:T(1024)(128)(4,1)S(1)}, s32[]{:S(2)}) async-start(s8[8388608]{0:T(1024)(128)(4,1)} %bitcast.30), calls=%async_computation.3 | async-start | bytes 8388608
  266.0 4.2 copy-start.11
  270.2 5.9 %copy-start.9 = (s32[9]{0:T(128)S(1)}, s32[9]{0:T(128)}, u32[]{:S(2)}) copy-start(s32[9]{0:T(128)} %param.13) | copy-start | bytes 112
  383.5 1.6 copy-start.1
  391.1 1.6 copy-start.3
  392.7 1.4 copy-start.4
  507.2 1.1 copy-start.5
Sparse Core Ops, SparseCore 0:
  225.9 89.5 reduce-scatter.1
where the time goes:
time: 549 us; the launch traced here: 544 us
  Pallas kernels  428 us (78%)
  matrix products  58.5 us (11%)
  starting transfers between devices  22.1 us (4%)
  between operations  19.7 us (4%)
  local copies, waits for them, and re-layouts  11.7 us (2%)
    pallas_call x2, Pallas kernels, swap(): pl.pallas_call(functools.partial(swap_kernel, peers, across // kinds, sha...  213 us
    pallas_call x1, Pallas kernels, spread(): pl.pallas_call(functools.partial(spread_kernel, peers, width), out_shape=...  180 us
    dot_general x10, matrix products, product(): lax.dot_general(left, right, (((left_dim,), (right_dim,)), ((), ())), pre...  58.5 us
    pallas_call x1, Pallas kernels, adam(): pl.pallas_call(adam_kernel, out_shape=[jax.ShapeDtypeStruct((kinds, capac...  27.6 us
    ppermute x1, starting transfers between devices, token_step(): lax.ppermute(straight, 'dp', [(i, i + 2) for i in range(0, devices - 2, 2)])  18 us
    unnamed x34, local copies, waits for them, and re-layouts  11.7 us
  transfers between devices with their start and end apart: 3, of which 0 were waited for; matrix products, arithmetic and copies ran while one was open for 7% of the time, Pallas kernels for 39%

commit v1 on v0

--- a/solution.py
+++ b/solution.py
@@ -343,6 +343,9 @@
 
     offsets = sorted(range(1, peers), key=lambda off: abs(2 * off - peers))
     share = -(-len(offsets) // planes)
+    for which in range(far.shape[0]):
+        for kind in range(kinds):
+            far_rows(which, kind).start()
     weights_out(offsets[:share])
 
     def share_on(which, shift, same):
@@ -372,10 +375,6 @@
 
                 each_z_in(step, receive)
         weights_out(offsets[share * step : share * (step + 1)])
-        if step == 1:
-            for which in range(far.shape[0]):
-                for kind in range(kinds):
-                    far_rows(which, kind).start()
 
     def everywhere(act):
         for step in range(planes):
@@ -464,13 +463,114 @@
     )(weights, tokens, upstream, far)
 
 
-def swap_kernel(peers, width, shares, *refs):
-    if shares:
-        packed, parts, arrived, gathered, send, recv, own_sem, p_send, p_recv, p_own = refs
-    else:
-        packed, arrived, send, recv, own_sem = refs
+def add_rows(target, left, right, step=256):
+    def some(number, carry):
+        here = pl.ds(pl.multiple_of(number * step, step), step)
+        total = left[here, :].astype(jnp.float32) + right[here, :].astype(jnp.float32)
+        target[here, :] = total.astype(target.dtype)
+        return carry
+
+    lax.fori_loop(0, target.shape[0] // step, some, 0)
+
+
+class Grads:
+    def __init__(self, peers, width, packed, arrived, send, recv, own_sem):
+        self.peers, self.width, self.packed, self.arrived = peers, width, packed, arrived
+        self.send, self.recv, self.own_sem = send, recv, own_sem
+        self.me = lax.axis_index("dp")
+        self.kinds = arrived.shape[0]
+
+    def place(self, dp, kind):
+        return self.arrived.at[kind, :, pl.ds(first_column(dp, self.width), self.width)]
+
+    def rows(self, peer, kind):
+        return self.packed.at[peer, :, pl.ds(kind * self.width, self.width)]
+
+    def out(self, off, kind):
+        peer = (self.me + off) % self.peers
+        return remote(
+            self.rows(peer, kind), self.place(self.me, kind),
+            self.send.at[off - 1, kind], self.recv.at[off - 1, kind], dp=peer,
+        )
+
+    def into(self, off, kind):
+        peer = (self.me + self.peers - off) % self.peers
+        here = self.place(peer, kind)
+        return remote(
+            here, here, self.send.at[off - 1, kind], self.recv.at[off - 1, kind], dp=peer
+        )
+
+    def own(self, kind):
+        return pltpu.make_async_copy(
+            self.rows(self.me, kind), self.place(self.me, kind), self.own_sem.at[kind]
+        )
+
+    def start(self):
+        @pl.when(self.me != IDLE)
+        def _():
+            for off in sorted(range(1, self.peers), key=lambda off: abs(2 * off - self.peers)):
+                for kind in range(self.kinds):
+                    self.out(off, kind).start()
+            for kind in range(self.kinds):
+                self.own(kind).start()
+
+    def wait(self):
+        for off in range(1, self.peers):
+            @pl.when((self.me + self.peers - off) % self.peers != IDLE)
+            def _():
+                for kind in range(self.kinds):
+                    self.into(off, kind).wait_recv()
+
+        @pl.when(self.me != IDLE)
+        def _():
+            for off in range(1, self.peers):
+                for kind in range(self.kinds):
+                    self.out(off, kind).wait_send()
+            for kind in range(self.kinds):
+                self.own(kind).wait()
+
+
+def swap_sum_kernel(peers, width, packed, partial, arrived, shares, send, recv, own_sem,
+                    from_core, both_cores, from_chip, c_send, c_recv, x_send, x_recv):
+    unit = lax.axis_index("mp")
+    core, chip = other_core(unit), other_chip(unit)
+    grads = Grads(peers, width, packed, arrived, send, recv, own_sem)
+    share = partial.shape[1] // 4
+    greet(peers)
+
+    def columns(unit):
+        return partial.at[:, pl.ds(pl.multiple_of(unit * share, share), share)]
+
+    def to_core(far):
+        whose = other_chip(core) if far else core
+        return remote(
+            columns(whose), from_core.at[far], c_send.at[far], c_recv.at[far], mp=core
+        )
+
+    across = remote(both_cores, from_chip, x_send, x_recv, mp=chip)
+    for far in (1, 0):
+        to_core(far).start()
+    grads.start()
+    to_core(1).wait_recv()
+    add_rows(both_cores, columns(chip), from_core.at[1])
+    to_core(0).wait_recv()
+    across.start()
+    add_rows(from_core.at[0], columns(unit), from_core.at[0])
+    across.wait_recv()
+    add_rows(shares, from_core.at[0], from_chip)
+    across.wait_send()
+    for far in (1, 0):
+        to_core(far).wait_send()
+    grads.wait()
+
+
+def swap_shares_kernel(peers, width, packed, shares, arrived, gathered, send, recv, own_sem,
+                       from_beside, both, y_send, y_recv, z_send, z_recv, keep_sem):
     me = lax.axis_index("dp")
-    kinds = arrived.shape[0]
+    z, y = me // 2, me % 2
+    planes = peers // 2
+    grads = Grads(peers, width, packed, arrived, send, recv, own_sem)
+    group = shares.shape[0] // peers
     barrier = pltpu.get_barrier_semaphore()
     for off in range(1, peers):
         pl.semaphore_signal(
@@ -481,94 +581,88 @@
         )
     pl.semaphore_wait(barrier, peers - 1)
 
-    def place(dp, kind):
-        return arrived.at[kind, :, pl.ds(first_column(dp, width), width)]
-
-    def out(off, kind):
-        peer = (me + off) % peers
-        return remote(
-            packed.at[peer, :, pl.ds(kind * width, width)], place(me, kind),
-            send.at[off - 1, kind], recv.at[off - 1, kind], dp=peer,
-        )
-
-    def into(off, kind):
-        peer = (me + peers - off) % peers
-        here = place(peer, kind)
-        return remote(here, here, send.at[off - 1, kind], recv.at[off - 1, kind], dp=peer)
-
-    def part(off):
-        peer = (me + off) % peers
-        return remote(
-            parts.at[peer], gathered.at[me], p_send.at[off - 1], p_recv.at[off - 1], dp=peer
-        )
-
-    def part_in(off):
-        peer = (me + peers - off) % peers
-        here = gathered.at[peer]
-        return remote(here, here, p_send.at[off - 1], p_recv.at[off - 1], dp=peer)
-
-    own = [
-        pltpu.make_async_copy(
-            packed.at[me, :, pl.ds(kind * width, width)], place(me, kind), own_sem.at[kind]
-        )
-        for kind in range(kinds)
-    ]
-    offsets = sorted(range(1, peers), key=lambda off: abs(2 * off - peers))
-    if shares:
-        own_part = pltpu.make_async_copy(parts.at[me], gathered.at[me], p_own)
-        for off in offsets:
-            part(off).start()
-        own_part.start()
-
-    @pl.when(me != IDLE)
-    def _():
-        for off in offsets:
-            for kind in range(kinds):
-                out(off, kind).start()
-        for copy in own:
-            copy.start()
-
-    if shares:
-        for off in offsets:
-            part_in(off).wait_recv()
-            part(off).wait_send()
-        own_part.wait()
-    for off in range(1, peers):
-        @pl.when((me + peers - off) % peers != IDLE)
-        def _():
-            for kind in range(kinds):
-                into(off, kind).wait_recv()
-
-    @pl.when(me != IDLE)
-    def _():
-        for off in range(1, peers):
-            for kind in range(kinds):
-                out(off, kind).wait_send()
-        for copy in own:
-            copy.wait()
-
-
-def swap(packed, kinds, columns, shares=None):
+    def rows(dp):
+        return shares.at[pl.ds(pl.multiple_of(dp * group, group), group)]
+
+    def along_y(plane):
+        return remote(
+            rows(plane * 2 + 1 - y), from_beside.at[plane],
+            y_send.at[plane], y_recv.at[plane], dp=z * 2 + 1 - y,
+        )
+
+    def along_z(by):
+        plane = (z + by) % planes
+        return remote(
+            both.at[plane], gathered.at[z], z_send.at[by - 1], z_recv.at[by - 1],
+            dp=plane * 2 + y,
+        )
+
+    def along_z_in(by):
+        plane = (z + planes - by) % planes
+        here = gathered.at[plane]
+        return remote(
+            here, here, z_send.at[by - 1], z_recv.at[by - 1], dp=plane * 2 + y
+        )
+
+    for plane in range(planes):
+        along_y(plane).start()
+    grads.start()
+    for plane in range(planes):
+        along_y(plane).wait_recv()
+        add_rows(both.at[plane], rows(plane * 2 + y), from_beside.at[plane])
+    keep = pltpu.make_async_copy(both.at[z], gathered.at[z], keep_sem)
+    for plane in range(planes):
+        along_y(plane).wait_send()
+    for by in range(1, planes):
+        along_z(by).start()
+    keep.start()
+    for by in range(1, planes):
+        along_z_in(by).wait_recv()
+        along_z(by).wait_send()
+    keep.wait()
+    grads.wait()
+
+
+def swap(kernel, packed, columns, kinds, other, gives, more, collective_id):
     peers, rows, across = packed.shape
     dma = pltpu.SemaphoreType.DMA
-    out_shape = [jax.ShapeDtypeStruct((kinds, rows, columns), packed.dtype)]
-    scratch = [dma((peers - 1, kinds)), dma((peers - 1, kinds)), dma((kinds,))]
-    operands = [packed]
-    if shares is not None:
-        operands.append(shares)
-        out_shape.append(jax.ShapeDtypeStruct(shares.shape, shares.dtype))
-        scratch += [dma((peers - 1,)), dma((peers - 1,)), dma]
     return pl.pallas_call(
-        functools.partial(swap_kernel, peers, across // kinds, shares is not None),
-        out_shape=out_shape,
-        in_specs=[WHOLE] * len(operands),
-        out_specs=[ANY] * len(out_shape),
-        scratch_shapes=scratch,
+        functools.partial(kernel, peers, across // kinds),
+        out_shape=[
+            jax.ShapeDtypeStruct((kinds, rows, columns), packed.dtype),
+            jax.ShapeDtypeStruct(gives, other.dtype),
+        ],
+        in_specs=[WHOLE] * 2,
+        out_specs=[ANY, WHOLE],
+        scratch_shapes=[dma((peers - 1, kinds)), dma((peers - 1, kinds)), dma((kinds,)), *more],
         compiler_params=pltpu.CompilerParams(
-            collective_id=1 + len(out_shape), has_side_effects=True, vmem_limit_bytes=16 << 20
+            collective_id=collective_id, has_side_effects=True, vmem_limit_bytes=40 << 20
         ),
         name="swap",
-    )(*operands)
+    )(packed, other)
+
+
+def swap_sum(packed, columns, kinds, partial):
+    rows, features = partial.shape
+    share = (rows, features // 4)
+    dma = pltpu.SemaphoreType.DMA
+    more = [
+        pltpu.VMEM((2, *share), partial.dtype),
+        pltpu.VMEM(share, partial.dtype),
+        pltpu.VMEM(share, partial.dtype),
+        dma((2,)), dma((2,)), dma, dma,
+    ]
+    return swap(swap_sum_kernel, packed, columns, kinds, partial, share, more, 1)
+
+
+def swap_shares(packed, columns, kinds, shares):
+    peers = packed.shape[0]
+    planes = peers // 2
+    landed = (planes, shares.shape[0] // peers, shares.shape[1])
+    dma = pltpu.SemaphoreType.DMA
+    more = [pltpu.VMEM(landed, shares.dtype)] * 2
+    more += [dma((planes,)), dma((planes,)), dma((planes - 1,)), dma((planes - 1,)), dma]
+    return swap(swap_shares_kernel, packed, columns, kinds, shares, landed, more, 2)
 
 
 STEP_ROWS = 40
@@ -686,6 +780,96 @@
     )(*states)
 
 
+def unpack_kernel(numbers, block, *refs):
+    rows, laid = refs[:-1], refs[-1]
+    owner = pl.program_id(0)
+    owners = pl.num_programs(0)
+    busy = numbers[owners + 1]
+    start = numbers[owner]
+    count = (numbers[owner + 1] - start) * busy
+    shift = start % 16
+    slots, width = block.shape[1], rows[0].shape[1]
+    window = (slots + 30) // 16 * 16
+
+    @pl.when(owner == 0)
+    def _():
+        laid[...] = jnp.zeros_like(laid)
+
+    slot = lax.broadcasted_iota(jnp.int32, block.shape[1:], 0)
+    values = jnp.where(slot < count, block[0], jnp.zeros_like(block[0]))
+    place = lax.broadcasted_iota(jnp.int32, (window, slots), 0) - shift
+    wanted = place == lax.broadcasted_iota(jnp.int32, (window, slots), 1)
+    found = jnp.dot(
+        wanted.astype(jnp.bfloat16), values, preferred_element_type=jnp.float32
+    ).astype(jnp.bfloat16)
+    here = pl.ds(pl.multiple_of(start - shift, 16), window)
+    laid[here, :] = laid[here, :] + found
+
+    @pl.when(owner == owners - 1)
+    def _():
+        for kind, row in enumerate(rows):
+            row[...] = laid[: row.shape[0], kind * width : (kind + 1) * width]
+
+
+def unpack(blocks, offsets, busy, features, kinds):
+    owners, slots, across = blocks.shape
+    width = across // kinds
+    whole = pl.BlockSpec((features, width), lambda owner, _: (0, 0))
+    return pl.pallas_call(
+        unpack_kernel,
+        out_shape=[jax.ShapeDtypeStruct((features, width), blocks.dtype)] * kinds,
+        grid_spec=pltpu.PrefetchScalarGridSpec(
+            num_scalar_prefetch=1,
+            grid=(owners,),
+            in_specs=[pl.BlockSpec((1, slots, across), lambda owner, _: (owner, 0, 0))],
+            out_specs=[whole] * kinds,
+            scratch_shapes=[pltpu.VMEM((features + slots + 24, across), blocks.dtype)],
+        ),
+        compiler_params=pltpu.CompilerParams(vmem_limit_bytes=24 << 20),
+        name="unpack",
+    )(jnp.concatenate([offsets, busy.astype(jnp.int32)[None]]), blocks)
+
+
+def pack_kernel(offsets, *refs):
+    grads, packed = refs[:-1], refs[-1]
+    features, width = grads[0].shape
+    slots = packed.shape[1]
+    window = (slots + 30) // 16 * 16
+    owner = pl.program_id(0)
+    start = offsets[owner]
+    count = offsets[owner + 1] - start
+    first = jnp.minimum(start - start % 16, features - window)
+    slot = lax.broadcasted_iota(jnp.int32, (slots, window), 0)
+    place = lax.broadcasted_iota(jnp.int32, (slots, window), 1)
+    wanted = ((place - slot == start - first) & (slot < count)).astype(jnp.bfloat16)
+    for kind, grad in enumerate(grads):
+        found = jnp.dot(
+            wanted,
+            grad[pl.ds(pl.multiple_of(first, 16), window), :],
+            preferred_element_type=jnp.float32,
+        )
+        packed[0, :, kind * width : (kind + 1) * width] = found.astype(packed.dtype)
+
+
+def pack(grads, offsets, slots):
+    features, width = grads[0].shape
+    owners = offsets.shape[0] - 1
+    across = len(grads) * width
+    whole = pl.BlockSpec((features, width), lambda owner, _: (0, 0))
+    return pl.pallas_call(
+        pack_kernel,
+        out_shape=jax.ShapeDtypeStruct((owners, slots, across), grads[0].dtype),
+        grid_spec=pltpu.PrefetchScalarGridSpec(
+            num_scalar_prefetch=1,
+            grid=(owners,),
+            in_specs=[whole] * len(grads),
+            out_specs=pl.BlockSpec((1, slots, across), lambda owner, _: (owner, 0, 0)),
+        ),
+        compiler_params=pltpu.CompilerParams(vmem_limit_bytes=24 << 20),
+        name="pack",
+    )(offsets, *grads)
+
+
 def lane_split(columns, peers):
     return -(-columns // (peers * 128)) * 128
 
@@ -702,7 +886,7 @@
 def token_pass(tokens, upstream, weights, far, old_offsets, new_offsets, capacity_new):
     peers = lax.axis_size("dp")
     feature_peers = lax.axis_size("mp")
-    kinds, capacity_old, columns = weights.shape
+    kinds, _, columns = weights.shape
     width = lane_split(columns, peers)
     features = tokens.shape[1]
     scale_in = features ** (-0.5)
@@ -712,14 +896,7 @@
     blocks, all_tokens, all_upstream, straight = spread(
         weights, tokens, upstream, far, peers, width
     )
-    blocks = blocks.reshape(peers * capacity_old, kinds * width)
-    target, in_range = row_layout(peers * capacity_old, capacity_old, old_offsets)
-    target = jnp.where(in_range, target, features)
-    wanted = jnp.arange(features, dtype=jnp.int32)[:, None] == target[None, :]
-    rows = product(wanted.astype(jnp.bfloat16), blocks, 1, 0)
-    rows = jnp.where(busy, rows, 0.0).astype(jnp.bfloat16)
-    rows = lax.optimization_barrier(rows)
-    rows = [rows[:, kind * width : (kind + 1) * width] for kind in range(kinds)]
+    rows = unpack(blocks, old_offsets, busy, features, kinds)
 
     gate_act = product(all_tokens, rows[0], 1, 0) * scale_in
     up_act = product(all_tokens, rows[1], 1, 0) * scale_in
@@ -732,28 +909,16 @@
     up_grad = (back_grad * gate_act * sigmoid_gate).astype(jnp.bfloat16)
 
     partial_value = (product(hidden, rows[2], 1, 1) * scale_hidden).astype(jnp.bfloat16)
-    partial_value = lax.psum_scatter(partial_value, "mp", scatter_dimension=1, tiled=True)
-    shares = partial_value.reshape(peers, -1, partial_value.shape[1])
-
-    target, in_range = row_layout(peers * capacity_new, capacity_new, new_offsets)
-    target = jnp.where(in_range, target, features)
-    wanted = target[:, None] == jnp.arange(features, dtype=jnp.int32)[None, :]
-    wanted = wanted.astype(jnp.bfloat16)
-
-    def packed(value):
-        value = lax.optimization_barrier(value)
-        value = product(wanted, value, 1, 0).astype(jnp.bfloat16)
-        return value.reshape(peers, capacity_new, -1)
 
     grads = [
         (product(all_tokens, gate_grad, 0, 0) * scale_in).astype(jnp.bfloat16),
         (product(all_tokens, up_grad, 0, 0) * scale_in).astype(jnp.bfloat16),
     ]
     last_grads = (product(all_upstream, hidden, 0, 0) * scale_hidden).astype(jnp.bfloat16)
-    first_packed = packed(jnp.concatenate(grads, axis=1))
-    last_packed = packed(last_grads)
-    (grads,) = swap(first_packed, kinds - 1, columns)
-    last_grads, shares = swap(last_packed, 1, columns, shares)
+    first_packed = pack(grads, new_offsets, capacity_new)
+    last_packed = pack([last_grads], new_offsets, capacity_new)
+    grads, shares = swap_sum(first_packed, columns, kinds - 1, partial_value)
+    last_grads, shares = swap_shares(last_packed, columns, 1, shares)
     layer_output = jnp.sum(shares.astype(jnp.float32), axis=0).astype(jnp.bfloat16)
     return grads, last_grads, layer_output, straight
 

time: 549 us -> 511 us (0.931)
  matrix products: 58.5 us -> 34.3 us
  starting transfers between devices: 22.1 us -> 6.33 us
  between operations: 19.7 us -> 6.06 us
  Pallas kernels: 428 us -> 436 us
  local copies, waits for them, and re-layouts: 11.7 us -> 19.1 us
    pallas_call x1, Pallas kernels: 180 us -> 255 us  [spread(): pl.pallas_call(functools.partial(spread_kernel, peers, width), out_shape=...]
    pallas_call x2 -> x5, Pallas kernels: 213 us -> 146 us  [the longest x2 135 us: swap(): pl.pallas_call(functools.partial(kernel, peers, across // kinds), out_sha...]
    dot_general x10 -> x7, matrix products: 58.5 us -> 34.3 us  [product(): lax.dot_general(left, right, (((left_dim,), (right_dim,)), ((), ())), pre...]
    ppermute x1, starting transfers between devices: 18 us -> 3.19 us  [token_step(): lax.ppermute(straight, 'dp', [(i, i + 2) for i in range(0, devices - 2, 2)])]
    unnamed x34 -> x48, local copies, waits for them, and re-layouts: 11.7 us -> 19.1 us
  transfers between devices with their start and end apart: 3 -> 2, of which waited for: 0 -> 0; matrix products, arithmetic and copies ran while one was open for 7% -> 7% of each run, Pallas kernels for 39% -> 79%
where the time goes in v1:
time: 511 us; the launch traced here: 505 us
  Pallas kernels  436 us (85%)
  matrix products  34.3 us (7%)
  local copies, waits for them, and re-layouts  19.1 us (4%)
  starting transfers between devices  6.33 us (1%)
  between operations  6.06 us (1%)
    pallas_call x1, Pallas kernels, spread(): pl.pallas_call(functools.partial(spread_kernel, peers, width), out_shape=...  255 us
    pallas_call x2, Pallas kernels, swap(): pl.pallas_call(functools.partial(kernel, peers, across // kinds), out_sha...  135 us
    dot_general x7, matrix products, product(): lax.dot_general(left, right, (((left_dim,), (right_dim,)), ((), ())), pre...  34.3 us
    pallas_call x1, Pallas kernels, adam(): pl.pallas_call(adam_kernel, out_shape=[jax.ShapeDtypeStruct((kinds, capac...  27.7 us
    unnamed x48, local copies, waits for them, and re-layouts  19.1 us
  transfers between devices with their start and end apart: 2, of which 0 were waited for; matrix products, arithmetic and copies ran while one was open for 7% of the time, Pallas kernels for 79%

profile of v1, /device:TPU:9, one launch (start us, length us, event | category | flops | bytes accessed | tf_op | source)
XLA Modules:
  0.0 504.7 jit_solution(12631465184437505894)
XLA Ops:
  0.6 2.8 copy-done
  3.4 8.2 %cast.1 = (bf16[3,3,152,1792]{3,2,1,0:T(8,128)(2,1)}, bf16[3,3,144,1792]{3,2,1,0:T(8,128)(2,1)S(1)}, bf16[3,296,1792]{2,1,0:T(8,128)(2,1)S(1)}) custom-call(f32[3,296,1792]{2,1,0:T(8,128)S(1)} %bitcast.24, f32[3,296,1792]{2,1,0:T(8,128)} %bitcast.29, f32[3,296,1792]{2,1,0:T(8,128)} %bitcast.31), custom_call_target="tpu_custom_call" | custom-call | tf_op jit(solution)/shard_map/cast/pallas_call | solution.py:767
  11.7 2.2 copy-done.1
  13.8 3.1 collective-permute-start
  20.2 2.3 copy-done.2
  22.6 254.6 %spread.1 = (bf16[8,296,768]{2,1,0:T(8,128)(2,1)S(1)}, bf16[2048,2048]{1,0:T(8,128)(2,1)S(1)}, bf16[2048,2048]{1,0:T(8,128)(2,1)}, bf16[3,3,144,1792]{3,2,1,0:T(8,128)(2,1)}) custom-call(bf16[3,296,1792]{2,1,0:T(8,128)(2,1)S(1)} %get-tuple-element.22.weights, bf16[256,2048]{1,0:T(8,128)(2,1)S(1)} %copy-done.7, ...), custom_call_target="tpu_custom_call" | custom-call | tf_op jit(solution)/shard_map/spread/pallas_call | solution.py:440
  277.2 1.8 copy-done.3
  279.0 3.2 copy-done.9
  282.2 3.2 collective-permute-start.1
  285.5 2.0 copy-done.4
  287.6 4.6 unpack.1
  292.2 6.3 %convolution_multiply_fusion.3 = f32[2048,256]{1,0:T(8,128)S(1)} fusion(bf16[2048,2048]{1,0:T(8,128)(2,1)} %copy-done.9, bf16[2048,256]{1,0:T(8,128)(2,1)S(1)} %get-tuple-element.30), kind=kOutput, calls=%fused_computation.4 | convolution fusion | flops 2148007936 | bytes 11534336 | tf_op jit(solution)/shard_map/dot_general | solution.py:878
  298.5 4.3 multiply_convert_fusion.1
  303.8 2.7 fusion.2.refs_0_
  310.3 2.9 pack.3.packed
  313.2 6.2 %convolution_multiply_fusion.5 = f32[2048,256]{1,0:T(8,128)S(1)} fusion(bf16[2048,2048]{1,0:T(8,128)(2,1)} %get-tuple-element.26, bf16[2048,256]{1,0:T(8,128)(2,1)} %copy-done.10), kind=kOutput, calls=%fused_computation.6 | convolution fusion | flops 2148007936 | bytes 11534336 | tf_op jit(solution)/shard_map/dot_general | solution.py:878
  319.4 6.3 %fusion.1.refs_1_ = bf16[2048,256]{1,0:T(8,128)(2,1)S(1)} fusion(bf16[2048,2048]{1,0:T(8,128)(2,1)} %copy-done.9, f32[2048,256]{1,0:T(8,128)S(1)} %convolution_multiply_fusion.5, f32[2048,256]{1,0:T(8,128)S(1)} %copy-done.16), kind=kOutput, calls=%fused_computation.8 | convolution fusion | flops 2151677952 | bytes 13631488 | tf_op jit(solution)/shard_map/dot_general | solution.py:878
  325.8 2.9 fusion.refs_0_
  328.7 3.6 pack.2.packed
  332.3 5.6 %multiply_convert_fusion.partial = bf16[2048,2048]{1,0:T(8,128)(2,1)} fusion(bf16[2048,256]{1,0:T(8,128)(2,1)S(1)} %copy-done.14, bf16[2048,256]{1,0:T(8,128)(2,1)S(1)} %copy-done.11), kind=kOutput, calls=%fused_computation | convolution fusion | flops 2155872256 | bytes 10485760 | tf_op jit(solution)/shard_map/dot_general | solution.py:878
  338.0 78.8 %swap.2 = (bf16[2,360,1792]{2,1,0:T(8,128)(2,1)S(1)}, bf16[2048,512]{1,0:T(8,128)(2,1)S(1)}) custom-call(bf16[8,360,512]{2,1,0:T(8,128)(2,1)S(1)} %pack.2.packed, bf16[2048,2048]{1,0:T(8,128)(2,1)} %multiply_convert_fusion.partial), custom_call_target="tpu_custom_call" | custom-call | tf_op jit(solution)/shard_map/swap/pallas_call | solution.py:629
  416.8 1.5 copy-done.5
  418.3 56.1 %swap.3 = (bf16[1,360,1792]{2,1,0:T(8,128)(2,1)S(1)}, bf16[4,256,512]{2,1,0:T(8,128)(2,1)S(1)}) custom-call(bf16[8,360,256]{2,1,0:T(8,128)(2,1)S(1)} %pack.3.packed, bf16[2048,512]{1,0:T(8,128)(2,1)S(1)} %get-tuple-element.32.shares), custom_call_target="tpu_custom_call" | custom-call | tf_op jit(solution)/shard_map/swap/pallas_call | solution.py:629
  477.1 27.7 %adam.1 = (f32[3,360,1792]{2,1,0:T(8,128)}, f32[3,360,1792]{2,1,0:T(8,128)}, f32[3,360,1792]{2,1,0:T(8,128)}) custom-call(s32[4]{0:T(128)} %pad_add_fusion.numbers, f32[3,296,1792]{2,1,0:T(8,128)} %bitcast.23, f32[3,296,1792]{2,1,0:T(8,128)} %bitcast.30, f32[3,296,1792]{2,1,0:T(8,128)} %bitcast.32, bf16[3,3,152,1792]{3,2,1,0:T(8,128)(2,1)} %collective-permute-done.refs_3_, ...), custom_call_target="tpu_custom_call" | custom-call | tf_op jit(solution)/shard_map/adam/pallas_call | solution.py:732
  (52 shorter events, 5.8 us)
Async XLA Ops:
  0.6 2.8 copy-start
  3.4 13.5 %copy-start.8 = (s32[9]{0:T(128)S(1)}, s32[9]{0:T(128)}, u32[]{:S(2)}) copy-start(s32[9]{0:T(128)} %offsets.3) | copy-start | bytes 112
  3.4 13.6 %copy-start.12 = (s32[9]{0:T(128)S(1)}, s32[9]{0:T(128)}, u32[]{:S(2)}) copy-start(s32[9]{0:T(128)} %param.12) | copy-start | bytes 112
  11.7 2.2 copy-start.1
  13.8 463.2 %collective-permute-start = (bf16[3,3,152,1792]{3,2,1,0:T(8,128)(2,1)}, bf16[3,3,152,1792]{3,2,1,0:T(8,128)(2,1)}, u32[]{:S(2)}, u32[]{:S(2)}) collective-permute-start(bf16[3,3,152,1792]{3,2,1,0:T(8,128)(2,1)} %get-tuple-element.21), channel_id=1, source_target_pairs={{0,4},{4,8},{8,12},{12,16},{16,20},{20,24},{24,28},{1,5},{5,9},{9,... | collective-permute-start | bytes 14708744 | tf_op jit(solution)/shard_map/ppermute | solution.py:944
  19.0 1.2 copy-start.7
  20.2 2.3 copy-start.2
  277.2 1.8 copy-start.3
  279.0 3.2 copy-start.9
  282.2 194.8 %collective-permute-start.1 = (bf16[3,3,144,1792]{3,2,1,0:T(8,128)(2,1)}, bf16[3,3,144,1792]{3,2,1,0:T(8,128)(2,1)}, u32[]{:S(2)}, u32[]{:S(2)}) collective-permute-start(bf16[3,3,144,1792]{3,2,1,0:T(8,128)(2,1)} %get-tuple-element.24.refs_4_), channel_id=1, source_target_pairs={{0,8},{8,16},{16,24},{1,9},{9,17},{17,25},{2,10},{10,18},{18,26},{... | collective-permute-start | bytes 13934600 | tf_op jit(solution)/shard_map/ppermute | solution.py:948
  285.5 2.0 copy-start.4
  287.6 10.9 %slice-start = ((s8[8388608]{0:T(1024)(128)(4,1)}), s8[4194304]{0:T(1024)(128)(4,1)S(1)}, s32[]{:S(2)}) async-start(s8[8388608]{0:T(1024)(128)(4,1)} %bitcast.25), calls=%async_computation | async-start | bytes 8388608
  292.2 6.3 %copy-start.10 = (bf16[2048,256]{1,0:T(8,128)(2,1)}, bf16[2048,256]{1,0:T(8,128)(2,1)S(1)}, u32[]{:S(2)}) copy-start(bf16[2048,256]{1,0:T(8,128)(2,1)S(1)} %get-tuple-element.28) | copy-start | bytes 3145732
  292.2 6.3 %slice-start.1 = ((s8[8388608]{0:T(1024)(128)(4,1)}), s8[4194304]{0:T(1024)(128)(4,1)S(1)}, s32[]{:S(2)}) async-start(s8[8388608]{0:T(1024)(128)(4,1)} %bitcast.25), calls=%async_computation.1 | async-start | bytes 8388608
  292.2 11.6 %slice-start.4 = ((s8[8388608]{0:T(1024)(128)(4,1)}), s8[4194304]{0:T(1024)(128)(4,1)S(1)}, s32[]{:S(2)}) async-start(s8[8388608]{0:T(1024)(128)(4,1)} %bitcast.33), calls=%async_computation.4 | async-start | bytes 8388608
  298.5 4.3 copy-start.15
  298.5 5.3 %slice-start.5 = ((s8[8388608]{0:T(1024)(128)(4,1)}), s8[4194304]{0:T(1024)(128)(4,1)S(1)}, s32[]{:S(2)}) async-start(s8[8388608]{0:T(1024)(128)(4,1)} %bitcast.33), calls=%async_computation.5 | async-start | bytes 8388608
  313.1 6.3 %copy-start.16 = (f32[2048,256]{1,0:T(8,128)S(1)}, f32[2048,256]{1,0:T(8,128)}, u32[]{:S(2)}) copy-start(f32[2048,256]{1,0:T(8,128)} %copy-done.15) | copy-start | bytes 6291460
  313.2 12.6 %slice-start.2 = ((s8[8388608]{0:T(1024)(128)(4,1)}), s8[4194304]{0:T(1024)(128)(4,1)S(1)}, s32[]{:S(2)}) async-start(s8[8388608]{0:T(1024)(128)(4,1)} %bitcast.27), calls=%async_computation.2 | async-start | bytes 8388608
  319.4 6.3 %slice-start.3 = ((s8[8388608]{0:T(1024)(128)(4,1)}), s8[4194304]{0:T(1024)(128)(4,1)S(1)}, s32[]{:S(2)}) async-start(s8[8388608]{0:T(1024)(128)(4,1)} %bitcast.27), calls=%async_computation.3 | async-start | bytes 8388608
  319.4 6.3 %copy-start.17 = (f32[2048,256]{1,0:T(8,128)S(1)}, f32[2048,256]{1,0:T(8,128)}, u32[]{:S(2)}) copy-start(f32[2048,256]{1,0:T(8,128)} %get-tuple-element.43) | copy-start | bytes 6291460
  328.7 3.6 copy-start.11
  328.7 3.6 copy-start.14
  416.8 1.5 copy-start.5
  (2 other events, 2.1 us)

commit v2 on v1

--- a/solution.py
+++ b/solution.py
@@ -199,8 +199,8 @@
     return (unit + 2) % 4
 
 
-def spread_kernel(peers, width, weights, tokens, upstream, far, blocks, all_tokens, all_upstream,
-                  crossed_far, w_send, w_recv, z_send, z_recv, y_send, y_recv, x_send, x_recv,
+def spread_kernel(peers, width, weights, tokens, upstream, far, near, blocks, all_tokens,
+                  all_upstream, crossed, crossed_rest, hopped, relayed, n_send, n_recv, w_send, w_recv, z_send, z_recv, y_send, y_recv, x_send, x_recv,
                   c_send, c_recv, f_send, f_recv, own_sem):
     me = lax.axis_index("dp")
     unit = lax.axis_index("mp")
@@ -300,9 +300,38 @@
 
     def far_rows(which, kind):
         return remote(
-            far.at[which, kind], crossed_far.at[which, kind],
+            far.at[which, kind], crossed_rest.at[which - 1, kind] if which else crossed.at[kind],
             f_send.at[which, kind], f_recv.at[which, kind], dp=beside,
         )
+
+    def hop(kind):
+        return remote(
+            near.at[kind], hopped.at[kind], n_send.at[kind], n_recv.at[kind], dp=(z + 1) * 2 + y
+        )
+
+    def hop_in(kind):
+        here = hopped.at[kind]
+        return remote(here, here, n_send.at[kind], n_recv.at[kind], dp=(z - 1) * 2 + y)
+
+    def relay(kind):
+        return remote(
+            crossed.at[kind], relayed.at[kind], n_send.at[kind], n_recv.at[kind],
+            dp=(z + 1) * 2 + y,
+        )
+
+    def relay_in(kind):
+        here = relayed.at[kind]
+        return remote(here, here, n_send.at[kind], n_recv.at[kind], dp=(z - 1) * 2 + y)
+
+    def each_hop(act, further):
+        for kind in range(kinds):
+            @pl.when(further & (y > 0))
+            def _():
+                act[0](kind)
+
+            @pl.when(further & (y == 0))
+            def _():
+                act[1](kind)
 
     up, down = z < planes - 1, z > 0
 
@@ -375,6 +404,10 @@
 
                 each_z_in(step, receive)
         weights_out(offsets[share * step : share * (step + 1)])
+
+    for kind in range(kinds):
+        far_rows(0, kind).wait_recv()
+    each_hop((lambda kind: hop(kind).start(), lambda kind: relay(kind).start()), up)
 
     def everywhere(act):
         for step in range(planes):
@@ -425,14 +458,20 @@
             for kind in range(kinds):
                 weight_in(off, kind).wait_recv()
 
+    each_hop((lambda kind: hop(kind).wait_send(), lambda kind: relay(kind).wait_send()), up)
+    each_hop(
+        (lambda kind: hop_in(kind).wait_recv(), lambda kind: relay_in(kind).wait_recv()), down
+    )
     for which in range(far.shape[0]):
         for kind in range(kinds):
-            far_rows(which, kind).wait()
+            far_rows(which, kind).wait_send()
+            if which:
+                far_rows(which, kind).wait_recv()
     for copy in own_rows:
         copy.wait()
 
 
-def spread(weights, tokens, upstream, far, peers, width):
+def spread(weights, tokens, upstream, far, near, peers, width):
     kinds, rows, _ = weights.shape
     group, features = tokens.shape
     planes = peers // 2
@@ -443,11 +482,15 @@
             jax.ShapeDtypeStruct((peers, rows, kinds * width), weights.dtype),
             jax.ShapeDtypeStruct((peers * group, features), tokens.dtype),
             jax.ShapeDtypeStruct((peers * group, features), tokens.dtype),
-            jax.ShapeDtypeStruct(far.shape, far.dtype),
+            jax.ShapeDtypeStruct(far.shape[1:], far.dtype),
+            jax.ShapeDtypeStruct((far.shape[0] - 1, *far.shape[1:]), far.dtype),
+            jax.ShapeDtypeStruct(near.shape, near.dtype),
+            jax.ShapeDtypeStruct(far.shape[1:], far.dtype),
         ),
-        in_specs=[WHOLE] * 3 + [ANY],
-        out_specs=[ANY] * 4,
+        in_specs=[WHOLE] * 3 + [ANY] * 2,
+        out_specs=[ANY] * 7,
         scratch_shapes=[
+            dma((kinds,)), dma((kinds,)),
             dma((peers - 1, kinds)), dma((peers - 1, kinds)),
             dma((2, 2 * planes, 2)), dma((2, 2 * planes, 2)),
             dma((2,)), dma((2,)),
@@ -460,7 +503,7 @@
             collective_id=0, has_side_effects=True, vmem_limit_bytes=24 << 20
         ),
         name="spread",
-    )(weights, tokens, upstream, far)
+    )(weights, tokens, upstream, far, near)
 
 
 def add_rows(target, left, right, step=256):
@@ -665,53 +708,81 @@
     return swap(swap_shares_kernel, packed, columns, kinds, shares, landed, more, 2)
 
 
-STEP_ROWS = 40
-
-
-def shifted(ref, which, start):
+STEP_ROWS = 72
+STEP_COLUMNS = 896
+
+
+def shifted(ref, which, start, cols):
     wide = STEP_ROWS + 8
     down = start % 8
-    rows = ref[which, pl.ds(pl.multiple_of(start - down, 8), wide), :]
+    rows = ref[which, pl.ds(pl.multiple_of(start - down, 8), wide), cols]
     rows = pltpu.roll(rows.reshape(wide // 8, 8, rows.shape[1]), 8 - down, 1)
     inside = lax.broadcasted_iota(jnp.int32, rows[1:].shape, 1) < 8 - down
     return jnp.where(inside, rows[:-1], rows[1:]).reshape(STEP_ROWS, rows.shape[2])
 
 
 def adam_kernel(numbers, *refs):
-    owns, near, straight, relayed, grads, last_grads = refs[:3], *refs[3:8]
-    outs, from_own, from_left = refs[8:11], refs[11], refs[12]
+    owns, nears, straights, relays = refs[:3], refs[3:5], refs[5:7], refs[7:9]
+    grads, last_grads, outs = *refs[9:11], refs[11:14]
+    from_own, from_left = refs[14:]
     arrived, left_skip, count, odd = numbers[0], numbers[1], numbers[2], numbers[3]
     capacity_old = owns[0].shape[1]
     capacity_new = outs[0].shape[1]
-    half = near.shape[2]
+    half = nears[0].shape[1]
+
+    def state(pair, which):
+        return pair[1][which - 1, 0] if which else pair[0][0]
+
     for which in range(3):
         from_own[which, pl.ds(capacity_new, capacity_old), :] = owns[which][0]
-        from_left[which, pl.ds(0, half), :] = near[which, 0].astype(jnp.float32)
+        from_left[which, pl.ds(0, half), :] = state(nears, which).astype(jnp.float32)
         far = pl.ds(half, capacity_old - half)
-        value = jnp.where(odd > 0, straight[which, 0], relayed[which, 0])
-        from_left[which, far, :] = value.astype(jnp.float32)
+
+        @pl.when(odd > 0)
+        def _():
+            from_left[which, far, :] = state(straights, which).astype(jnp.float32)
+
+        @pl.when(odd == 0)
+        def _():
+            from_left[which, far, :] = state(relays, which).astype(jnp.float32)
+
     kinds = pl.num_programs(0)
     is_last = pl.program_id(0) == kinds - 1
 
+    pieces = outs[0].shape[2] // STEP_COLUMNS
+
     def some_rows(step, carry):
-        first = pl.multiple_of(step * STEP_ROWS, 8)
-        slot = first + lax.broadcasted_iota(jnp.int32, (STEP_ROWS, outs[0].shape[2]), 0)
-        rows = [
-            jnp.where(
-                slot < arrived,
-                shifted(from_left, which, first + left_skip),
-                shifted(from_own, which, first + capacity_new - arrived),
-            )
-            for which in range(3)
-        ]
+        first = pl.multiple_of(step // pieces * STEP_ROWS, 8)
         here = pl.ds(first, STEP_ROWS)
-        grad = jnp.where(is_last, last_grads[0, here, :], grads[0, here, :]).astype(jnp.float32)
-        updated = adam_step(rows[0], rows[1], rows[2], grad)
-        for which in range(3):
-            outs[which][0, here, :] = jnp.where(slot < count, updated[which], 0.0)
+        cols = pl.ds(pl.multiple_of(step % pieces * STEP_COLUMNS, 128), STEP_COLUMNS)
+        slot = first + lax.broadcasted_iota(jnp.int32, (STEP_ROWS, STEP_COLUMNS), 0)
+
+        def finish(rows):
+            grad = jnp.where(is_last, last_grads[0, here, cols], grads[0, here, cols])
+            updated = adam_step(rows[0], rows[1], rows[2], grad.astype(jnp.float32))
+            for which in range(3):
+                outs[which][0, here, cols] = jnp.where(slot < count, updated[which], 0.0)
+
+        own = first + capacity_new - arrived
+
+        @pl.when(first < arrived)
+        def _():
+            finish([
+                jnp.where(
+                    slot < arrived,
+                    shifted(from_left, which, first + left_skip, cols),
+                    shifted(from_own, which, own, cols),
+                )
+                for which in range(3)
+            ])
+
+        @pl.when(first >= arrived)
+        def _():
+            finish([shifted(from_own, which, own, cols) for which in range(3)])
+
         return carry
 
-    lax.fori_loop(0, capacity_new // STEP_ROWS, some_rows, 0)
+    lax.fori_loop(0, capacity_new // STEP_ROWS * pieces, some_rows, 0)
 
 
 def adam(states, moved, grads, last_grads, numbers):
@@ -722,8 +793,15 @@
     def block(rows):
         return pl.BlockSpec((1, rows, width), lambda kind, part, _: (kind, 0, part))
 
-    def stacked(rows):
-        return pl.BlockSpec((3, 1, rows, width), lambda kind, part, _: (0, kind, 0, part))
+    def given(value, parity):
+        def used(numbers):
+            return 1 if parity is None else 1 - (numbers[3] - parity) * (numbers[3] - parity)
+
+        if value.ndim == 3:
+            shape = (1, value.shape[1], width)
+            return pl.BlockSpec(shape, lambda kind, part, n: (kind * used(n), 0, part * used(n)))
+        shape = (2, 1, value.shape[2], width)
+        return pl.BlockSpec(shape, lambda kind, part, n: (0, kind * used(n), 0, part * used(n)))
 
     first_grads = pl.BlockSpec(
         (1, capacity_new, width), lambda kind, part, _: (jnp.minimum(kind, kinds - 2), 0, part)
@@ -736,7 +814,7 @@
             num_scalar_prefetch=1,
             grid=(kinds, columns // width),
             in_specs=[block(capacity_old)] * 3
-            + [stacked(value.shape[2]) for value in moved]
+            + [given(value, parity) for pair, parity in zip(moved, (None, 1, 0)) for value in pair]
             + [first_grads, third_grads],
             out_specs=[block(capacity_new)] * 3,
             scratch_shapes=[
@@ -746,14 +824,15 @@
         ),
         compiler_params=pltpu.CompilerParams(vmem_limit_bytes=60 << 20),
         name="adam",
-    )(numbers, *states, *moved, grads, last_grads)
+    )(numbers, *states, *(value for pair in moved for value in pair), grads, last_grads)
 
 
 def cast_kernel(*refs):
-    owns, near, far, weights = refs[:3], refs[3], refs[4], refs[5]
-    half = near.shape[2]
+    owns, near, near_rest, far, weights = refs[:3], *refs[3:]
+    half = near.shape[1]
     for which in range(3):
-        near[which, 0] = owns[which][0, :half, :].astype(near.dtype)
+        target = near_rest.at[which - 1, 0] if which else near.at[0]
+        target[...] = owns[which][0, :half, :].astype(near.dtype)
         far[which, 0] = owns[which][0, half:, :].astype(far.dtype)
     weights[0] = owns[0][0].astype(weights.dtype)
 
@@ -762,19 +841,25 @@
     kinds, rows, columns = states[0].shape
     width = columns // 2 if columns % 256 == 0 else columns
     half = (rows + 15) // 16 * 8
-    stacked = [(3, kinds, half, columns), (3, kinds, rows - half, columns)]
-    whole = pl.BlockSpec((1, rows, width), lambda kind, part: (kind, 0, part))
+
+    def one(rows):
+        return pl.BlockSpec((1, rows, width), lambda kind, part: (kind, 0, part))
+
+    def several(count, rows):
+        return pl.BlockSpec((count, 1, rows, width), lambda kind, part: (0, kind, 0, part))
+
+    shapes = [
+        (kinds, half, columns),
+        (2, kinds, half, columns),
+        (3, kinds, rows - half, columns),
+        (kinds, rows, columns),
+    ]
     return pl.pallas_call(
         cast_kernel,
-        out_shape=[jax.ShapeDtypeStruct(shape, jnp.bfloat16) for shape in stacked]
-        + [jax.ShapeDtypeStruct(states[0].shape, jnp.bfloat16)],
+        out_shape=[jax.ShapeDtypeStruct(shape, jnp.bfloat16) for shape in shapes],
         grid=(kinds, columns // width),
-        in_specs=[whole] * 3,
-        out_specs=[
-            pl.BlockSpec((3, 1, shape[2], width), lambda kind, part: (0, kind, 0, part))
-            for shape in stacked
-        ]
-        + [whole],
+        in_specs=[one(rows)] * 3,
+        out_specs=[one(half), several(2, half), several(3, rows - half), one(rows)],
         compiler_params=pltpu.CompilerParams(vmem_limit_bytes=32 << 20),
         name="cast",
     )(*states)
@@ -883,7 +968,7 @@
     )
 
 
-def token_pass(tokens, upstream, weights, far, old_offsets, new_offsets, capacity_new):
+def token_pass(tokens, upstream, weights, far, near, old_offsets, new_offsets, capacity_new):
     peers = lax.axis_size("dp")
     feature_peers = lax.axis_size("mp")
     kinds, _, columns = weights.shape
@@ -893,8 +978,8 @@
     scale_hidden = (columns * feature_peers) ** (-0.5)
     busy = lax.axis_index("dp") != IDLE
 
-    blocks, all_tokens, all_upstream, straight = spread(
-        weights, tokens, upstream, far, peers, width
+    blocks, all_tokens, all_upstream, *arrived = spread(
+        weights, tokens, upstream, far, near, peers, width
     )
     rows = unpack(blocks, old_offsets, busy, features, kinds)
 
@@ -907,6 +992,7 @@
         back_grad * up_act * sigmoid_gate * (1.0 + gate_act * (1.0 - sigmoid_gate))
     ).astype(jnp.bfloat16)
     up_grad = (back_grad * gate_act * sigmoid_gate).astype(jnp.bfloat16)
+    gate_grad, up_grad = lax.optimization_barrier((gate_grad, up_grad))
 
     partial_value = (product(hidden, rows[2], 1, 1) * scale_hidden).astype(jnp.bfloat16)
 
@@ -920,7 +1006,7 @@
     grads, shares = swap_sum(first_packed, columns, kinds - 1, partial_value)
     last_grads, shares = swap_shares(last_packed, columns, 1, shares)
     layer_output = jnp.sum(shares.astype(jnp.float32), axis=0).astype(jnp.bfloat16)
-    return grads, last_grads, layer_output, straight
+    return grads, last_grads, layer_output, arrived
 
 
 def token_body(*arguments):
@@ -940,13 +1026,17 @@
     upstream = jnp.where(live_flag, out_grad, jnp.zeros_like(out_grad))
 
     states = [value.transpose(1, 0, 2) for value in (master, moment_one, moment_two)]
-    near, far, weights = cast(states)
-    near = lax.ppermute(near, "dp", [(i, i + 1) for i in range(devices - 1)])
-    grads, last_grads, layer_output, straight = token_pass(
-        tokens, upstream, weights, far, old_offsets, new_offsets, capacity_new
-    )
-    relayed = lax.ppermute(straight, "dp", [(i, i + 2) for i in range(0, devices - 2, 2)])
-    moved = (near, straight, relayed)
+    near, near_rest, far, weights = cast(states)
+    near_rest = lax.ppermute(near_rest, "dp", [(i, i + 1) for i in range(devices - 1)])
+    grads, last_grads, layer_output, landed = token_pass(
+        tokens, upstream, weights, far, near, old_offsets, new_offsets, capacity_new
+    )
+    straight, straight_rest, hopped, relayed = landed
+    pairs = [(i, i + 1 - 2 * (i % 2)) for i in range(devices) if i != 1]
+    near = lax.ppermute(jnp.where(device_index % 2 > 0, hopped, near), "dp", pairs)
+    pairs = [(i, i + 2) for i in range(0, devices - 2, 2)]
+    relayed_rest = lax.ppermute(straight_rest, "dp", pairs)
+    moved = ((near, near_rest), (straight, straight_rest), (relayed, relayed_rest))
     arrived = jnp.clip(old_start - new_start, 0, capacity_new)
     left_skip = jnp.clip(new_start - left_start, 0, capacity_old)
     numbers = jnp.stack([arrived, left_skip, new_end - new_start, device_index % 2])
@@ -973,6 +1063,7 @@
         and tokens.shape[0] % 64 == 0
         and columns == (devices - 1) * lane_split(columns, devices)
         and new_capacity(tokens.shape[1], devices) % STEP_ROWS == 0
+        and columns % (2 * STEP_COLUMNS) == 0
     )
     chosen = token_body if whole and moved_tokens <= moved_rows else body
     return chosen(tokens, out_grad, master, *others)

time: 511 us -> 486 us (0.951)
  Pallas kernels: 436 us -> 397 us
  starting transfers between devices: 6.33 us -> 24.5 us
    pallas_call x1, Pallas kernels: 255 us -> 219 us  [spread(): pl.pallas_call(functools.partial(spread_kernel, peers, width), out_shape=...]
    ppermute x2 -> x3, starting transfers between devices: 6.33 us -> 24.5 us  [the longest x1 12.7 us: token_step(): relayed_rest = lax.ppermute(straight_rest, 'dp', pairs)]
    unnamed x48 -> x42, local copies, waits for them, and re-layouts: 19.1 us -> 18.6 us
  transfers between devices with their start and end apart: 2 -> 3, of which waited for: 0 -> 0; matrix products, arithmetic and copies ran while one was open for 7% -> 8% of each run, Pallas kernels for 79% -> 75%
where the time goes in v2:
time: 486 us; the launch traced here: 484 us
  Pallas kernels  397 us (82%)
  matrix products  33.7 us (7%)
  starting transfers between devices  24.5 us (5%)
  local copies, waits for them, and re-layouts  18.6 us (4%)
  between operations  6.33 us (1%)
    pallas_call x1, Pallas kernels, spread(): pl.pallas_call(functools.partial(spread_kernel, peers, width), out_shape=...  219 us
    pallas_call x2, Pallas kernels, swap(): pl.pallas_call(functools.partial(kernel, peers, across // kinds), out_sha...  134 us
    dot_general x7, matrix products, product(): lax.dot_general(left, right, (((left_dim,), (right_dim,)), ((), ())), pre...  33.7 us
    pallas_call x1, Pallas kernels, adam(): pl.pallas_call(adam_kernel, out_shape=[jax.ShapeDtypeStruct((kinds, capac...  25.2 us
    unnamed x42, local copies, waits for them, and re-layouts  18.6 us
    ppermute x1, starting transfers between devices, token_step(): relayed_rest = lax.ppermute(straight_rest, 'dp', pairs)  12.7 us
  transfers between devices with their start and end apart: 3, of which 0 were waited for; matrix products, arithmetic and copies ran while one was open for 8% of the time, Pallas kernels for 75%

profile of v2, /device:TPU:9, one launch (start us, length us, event | category | flops | bytes accessed | tf_op | source)
XLA Modules:
  0.0 484.5 jit_solution(8913649061861610833)
XLA Ops:
  0.6 2.8 copy-done
  3.4 7.8 %cast.1 = (bf16[3,152,1792]{2,1,0:T(8,128)(2,1)S(1)}, bf16[2,3,152,1792]{3,2,1,0:T(8,128)(2,1)}, bf16[3,3,144,1792]{3,2,1,0:T(8,128)(2,1)S(1)}, bf16[3,296,1792]{2,1,0:T(8,128)(2,1)S(1)}) custom-call(f32[3,296,1792]{2,1,0:T(8,128)S(1)} %bitcast.26, f32[3,296,1792]{2,1,0:T(8,128)} %bitcast.27, f32[3,296,1792]{2,1,0:T(8,128)} %bitcast.29), custom_call_target="tpu_custom_call" | custom-call | tf_op jit(solution)/shard_map/cast/pallas_call | solution.py:857
  11.3 2.2 copy-done.1
  13.4 1.7 copy-done.5
  15.1 3.3 collective-permute-start.1
  20.6 2.3 copy-done.2
  22.9 1.9 copy-done.6
  24.8 218.9 %spread.1 = (bf16[8,296,768]{2,1,0:T(8,128)(2,1)S(1)}, bf16[2048,2048]{1,0:T(8,128)(2,1)}, bf16[2048,2048]{1,0:T(8,128)(2,1)}, bf16[3,144,1792]{2,1,0:T(8,128)(2...) custom-call(bf16[3,296,1792]{2,1,0:T(8,128)(2,1)S(1)} %copy-done.6, ...), custom_call_target="tpu_custom_call" | custom-call | tf_op jit(solution)/shard_map/spread/pallas_call | solution.py:479
  248.4 8.5 %collective-permute-start = (bf16[3,152,1792]{2,1,0:T(8,128)(2,1)}, bf16[3,152,1792]{2,1,0:T(8,128)(2,1)}, u32[]{:S(2)}, u32[]{:S(2)}) collective-permute-start(bf16[3,152,1792]{2,1,0:T(8,128)(2,1)} %broadcast_select_fusion), channel_id=1, source_target_pairs={{0,4},{8,12},{12,8},{16,20},{20,16},{24,28},{28,24},{1,5},{9,13},{... | collective-permute-start | bytes 4902920 | tf_op jit(solution)/shard_map/ppermute | solution.py:1036
  256.9 12.7 %collective-permute-start.2 = (bf16[2,3,144,1792]{3,2,1,0:T(8,128)(2,1)}, bf16[2,3,144,1792]{3,2,1,0:T(8,128)(2,1)}, u32[]{:S(2)}, u32[]{:S(2)}) collective-permute-start(bf16[2,3,144,1792]{3,2,1,0:T(8,128)(2,1)} %get-tuple-element.33.refs_6_), channel_id=1, source_target_pairs={{0,8},{8,16},{16,24},{1,9},{9,17},{17,25},{2,10},{10,18},{18,26},{... | collective-permute-start | bytes 9289736 | tf_op jit(solution)/shard_map/ppermute | solution.py:1038
  274.4 2.0 copy-done.4
  276.4 4.6 unpack.1
  281.0 6.0 %convolution_multiply_fusion.3 = f32[2048,256]{1,0:T(8,128)S(1)} fusion(bf16[2048,2048]{1,0:T(8,128)(2,1)} %get-tuple-element.35, bf16[2048,256]{1,0:T(8,128)(2,1)S(1)} %get-tuple-element.40), kind=kOutput, calls=%fused_computation.4 | convolution fusion | flops 2148007936 | bytes 11534336 | tf_op jit(solution)/shard_map/dot_general | solution.py:963
  287.1 2.4 convolution_multiply_fusion.5
  289.5 4.9 %multiply_convert_fusion.1 = (bf16[2048,256]{1,0:T(8,128)(2,1)S(1)}, bf16[2048,256]{1,0:T(8,128)(2,1)}, bf16[2048,256]{1,0:T(8,128)(2,1)}) fusion(f32[2048,256]{1,0:T(8,128)S(1)} %convolution_multiply_fusion.3, f32[2048,256]{1,0:T(8,128)S(1)} %convolution_multiply_fusion.5, bf16[2048,2048]{1,0:T(8,128)(2,1)S(1)} %bitcast.32, ...), kind=kOutput, calls=%fused_computation.10 | convolution fusion | flops 2156396544 | bytes 16777216 | tf_op jit(solution)/shard_map/dot_general | solution.py:963
  294.4 2.7 fusion.2.refs_0_
  297.1 2.9 pack.3.packed
  300.0 6.2 %fusion.refs_0_ = bf16[2048,256]{1,0:T(8,128)(2,1)S(1)} fusion(bf16[2048,2048]{1,0:T(8,128)(2,1)} %get-tuple-element.35, bf16[2048,256]{1,0:T(8,128)(2,1)} %get-tuple-element.41), kind=kOutput, calls=%fused_computation.7 | convolution fusion | flops 2148532224 | bytes 10485760 | tf_op jit(solution)/shard_map/dot_general | solution.py:963
  306.2 5.9 %fusion.1.refs_1_ = bf16[2048,256]{1,0:T(8,128)(2,1)S(1)} fusion(bf16[2048,2048]{1,0:T(8,128)(2,1)} %get-tuple-element.35, bf16[2048,256]{1,0:T(8,128)(2,1)S(1)} %copy-done.16), kind=kOutput, calls=%fused_computation.8 | convolution fusion | flops 2148532224 | bytes 10485760 | tf_op jit(solution)/shard_map/dot_general | solution.py:963
  312.2 3.6 pack.2.packed
  315.7 5.6 %multiply_convert_fusion.partial = bf16[2048,2048]{1,0:T(8,128)(2,1)} fusion(bf16[2048,256]{1,0:T(8,128)(2,1)S(1)} %copy-done.15, bf16[2048,256]{1,0:T(8,128)(2,1)S(1)} %get-tuple-element.38), kind=kOutput, calls=%fused_computation | convolution fusion | flops 2155872256 | bytes 10485760 | tf_op jit(solution)/shard_map/dot_general | solution.py:963
  321.4 65.4 %swap.2 = (bf16[2,360,1792]{2,1,0:T(8,128)(2,1)S(1)}, bf16[2048,512]{1,0:T(8,128)(2,1)S(1)}) custom-call(bf16[8,360,512]{2,1,0:T(8,128)(2,1)S(1)} %pack.2.packed, bf16[2048,2048]{1,0:T(8,128)(2,1)} %multiply_convert_fusion.partial), custom_call_target="tpu_custom_call" | custom-call | tf_op jit(solution)/shard_map/swap/pallas_call | solution.py:672
  388.3 68.3 %swap.3 = (bf16[1,360,1792]{2,1,0:T(8,128)(2,1)S(1)}, bf16[4,256,512]{2,1,0:T(8,128)(2,1)S(1)}) custom-call(bf16[8,360,256]{2,1,0:T(8,128)(2,1)S(1)} %pack.3.packed, bf16[2048,512]{1,0:T(8,128)(2,1)S(1)} %get-tuple-element.44.shares), custom_call_target="tpu_custom_call" | custom-call | tf_op jit(solution)/shard_map/swap/pallas_call | solution.py:672
  459.2 25.2 %adam.1 = (f32[3,360,1792]{2,1,0:T(8,128)}, f32[3,360,1792]{2,1,0:T(8,128)}, f32[3,360,1792]{2,1,0:T(8,128)}) custom-call(s32[4]{0:T(128)} %pad_add_fusion.numbers, f32[3,296,1792]{2,1,0:T(8,128)} %bitcast.25, f32[3,296,1792]{2,1,0:T(8,128)} %bitcast.28, f32[3,296,1792]{2,1,0:T(8,128)} %bitcast.30, bf16[3,152,1792]{2,1,0:T(8,128)(2,1)} %collective-permute-done.refs_3_, ...), custom_call_target="tpu_custom_call" | custom-call | tf_op jit(solution)/shard_map/adam/pallas_call | solution.py:810
  (49 shorter events, 10.4 us)
Async XLA Ops:
  0.6 2.8 copy-start
  3.4 15.0 %copy-start.12 = (s32[9]{0:T(128)S(1)}, s32[9]{0:T(128)}, u32[]{:S(2)}) copy-start(s32[9]{0:T(128)} %offsets.3) | copy-start | bytes 112
  11.3 2.2 copy-start.1
  13.4 1.7 copy-start.5
  15.1 5.4 %copy-start.11 = (bf16[256,2048]{1,0:T(8,128)(2,1)S(1)}, bf16[256,2048]{1,0:T(8,128)(2,1)}, u32[]{:S(2)}) copy-start(bf16[256,2048]{1,0:T(8,128)(2,1)} %tokens.1) | copy-start | bytes 3145732
  15.1 444.1 %collective-permute-start.1 = (bf16[2,3,152,1792]{3,2,1,0:T(8,128)(2,1)}, bf16[2,3,152,1792]{3,2,1,0:T(8,128)(2,1)}, u32[]{:S(2)}, u32[]{:S(2)}) collective-permute-start(bf16[2,3,152,1792]{3,2,1,0:T(8,128)(2,1)} %get-tuple-element.31), channel_id=1, source_target_pairs={{0,4},{4,8},{8,12},{12,16},{16,20},{20,24},{24,28},{1,5},{5,9},{9,... | collective-permute-start | bytes 9805832 | tf_op jit(solution)/shard_map/ppermute | solution.py:1030
  20.6 2.3 copy-start.2
  22.9 1.9 copy-start.6
  243.6 1.2 copy-start.8
  244.8 1.2 copy-start.9
  246.0 2.4 copy-start.3
  246.0 24.9 %copy-start.13 = (s32[9]{0:T(128)S(1)}, s32[9]{0:T(128)}, u32[]{:S(2)}) copy-start(s32[9]{0:T(128)} %param.12) | copy-start | bytes 112
  248.4 210.9 %collective-permute-start = (bf16[3,152,1792]{2,1,0:T(8,128)(2,1)}, bf16[3,152,1792]{2,1,0:T(8,128)(2,1)}, u32[]{:S(2)}, u32[]{:S(2)}) collective-permute-start(bf16[3,152,1792]{2,1,0:T(8,128)(2,1)} %broadcast_select_fusion), channel_id=1, source_target_pairs={{0,4},{8,12},{12,8},{16,20},{20,16},{24,28},{28,24},{1,5},{9,13},{... | collective-permute-start | bytes 4902920 | tf_op jit(solution)/shard_map/ppermute | solution.py:1036
  256.9 202.3 %collective-permute-start.2 = (bf16[2,3,144,1792]{3,2,1,0:T(8,128)(2,1)}, bf16[2,3,144,1792]{3,2,1,0:T(8,128)(2,1)}, u32[]{:S(2)}, u32[]{:S(2)}) collective-permute-start(bf16[2,3,144,1792]{3,2,1,0:T(8,128)(2,1)} %get-tuple-element.33.refs_6_), channel_id=1, source_target_pairs={{0,8},{8,16},{16,24},{1,9},{9,17},{17,25},{2,10},{10,18},{18,26},{... | collective-permute-start | bytes 9289736 | tf_op jit(solution)/shard_map/ppermute | solution.py:1038
  274.4 2.0 copy-start.4
  276.4 10.6 %slice-start.2 = ((s8[8388608]{0:T(1024)(128)(4,1)}), s8[4194304]{0:T(1024)(128)(4,1)S(1)}, s32[]{:S(2)}) async-start(s8[8388608]{0:T(1024)(128)(4,1)} %bitcast.33), calls=%async_computation.2 | async-start | bytes 8388608
  281.0 6.0 %slice-start.3 = ((s8[8388608]{0:T(1024)(128)(4,1)}), s8[4194304]{0:T(1024)(128)(4,1)S(1)}, s32[]{:S(2)}) async-start(s8[8388608]{0:T(1024)(128)(4,1)} %bitcast.33), calls=%async_computation.3 | async-start | bytes 8388608
  281.0 8.5 %slice-start = ((s8[8388608]{0:T(1024)(128)(4,1)}), s8[4194304]{0:T(1024)(128)(4,1)S(1)}, s32[]{:S(2)}) async-start(s8[8388608]{0:T(1024)(128)(4,1)} %bitcast.31), calls=%async_computation | async-start | bytes 8388608
  287.0 2.5 slice-start.1
  294.4 2.7 copy-start.14
  300.0 6.2 %copy-start.16 = (bf16[2048,256]{1,0:T(8,128)(2,1)S(1)}, bf16[2048,256]{1,0:T(8,128)(2,1)}, u32[]{:S(2)}) copy-start(bf16[2048,256]{1,0:T(8,128)(2,1)} %get-tuple-element.42) | copy-start | bytes 3145732
  312.2 3.6 copy-start.15
  386.8 1.5 copy-start.7
  456.6 1.1 copy-start.10

commit v3 on v2

--- a/solution.py
+++ b/solution.py
@@ -199,8 +199,9 @@
     return (unit + 2) % 4
 
 
-def spread_kernel(peers, width, weights, tokens, upstream, far, near, blocks, all_tokens,
-                  all_upstream, crossed, crossed_rest, hopped, relayed, n_send, n_recv, w_send, w_recv, z_send, z_recv, y_send, y_recv, x_send, x_recv,
+def spread_kernel(peers, width, weights, tokens, upstream, far, near, first, second, blocks,
+                  all_tokens, all_upstream, crossed, crossed_rest, hopped, relayed, near_rest,
+                  far_rest, n_send, n_recv, w_send, w_recv, z_send, z_recv, y_send, y_recv, x_send, x_recv,
                   c_send, c_recv, f_send, f_recv, own_sem):
     me = lax.axis_index("dp")
     unit = lax.axis_index("mp")
@@ -300,7 +301,8 @@
 
     def far_rows(which, kind):
         return remote(
-            far.at[which, kind], crossed_rest.at[which - 1, kind] if which else crossed.at[kind],
+            far_rest.at[which - 1, kind] if which else far.at[kind],
+            crossed_rest.at[which - 1, kind] if which else crossed.at[kind],
             f_send.at[which, kind], f_recv.at[which, kind], dp=beside,
         )
 
@@ -372,10 +374,30 @@
 
     offsets = sorted(range(1, peers), key=lambda off: abs(2 * off - peers))
     share = -(-len(offsets) // planes)
-    for which in range(far.shape[0]):
+    for kind in range(kinds):
+        far_rows(0, kind).start()
+    weights_out(offsets[:share])
+
+    half, rest = near_rest.shape[2], far_rest.shape[2]
+    across = first.shape[2] // 2
+
+    def halves(*refs):
+        for which in range(2):
+            refs[2][which, 0] = refs[which][0, :half, :].astype(near_rest.dtype)
+            refs[3][which, 0] = refs[which][0, half:, :].astype(far_rest.dtype)
+
+    pltpu.emit_pipeline(
+        halves,
+        grid=(kinds, 2),
+        in_specs=[pl.BlockSpec((1, half + rest, across), lambda kind, part: (kind, 0, part))] * 2,
+        out_specs=[
+            pl.BlockSpec((2, 1, count, across), lambda kind, part: (0, kind, 0, part))
+            for count in (half, rest)
+        ],
+    )(first, second, near_rest, far_rest)
+    for which in range(1, 3):
         for kind in range(kinds):
             far_rows(which, kind).start()
-    weights_out(offsets[:share])
 
     def share_on(which, shift, same):
         along_x(which, shift, same).start()
@@ -462,7 +484,7 @@
     each_hop(
         (lambda kind: hop_in(kind).wait_recv(), lambda kind: relay_in(kind).wait_recv()), down
     )
-    for which in range(far.shape[0]):
+    for which in range(3):
         for kind in range(kinds):
             far_rows(which, kind).wait_send()
             if which:
@@ -471,7 +493,7 @@
         copy.wait()
 
 
-def spread(weights, tokens, upstream, far, near, peers, width):
+def spread(weights, tokens, upstream, far, near, others, peers, width):
     kinds, rows, _ = weights.shape
     group, features = tokens.shape
     planes = peers // 2
@@ -482,13 +504,15 @@
             jax.ShapeDtypeStruct((peers, rows, kinds * width), weights.dtype),
             jax.ShapeDtypeStruct((peers * group, features), tokens.dtype),
             jax.ShapeDtypeStruct((peers * group, features), tokens.dtype),
-            jax.ShapeDtypeStruct(far.shape[1:], far.dtype),
-            jax.ShapeDtypeStruct((far.shape[0] - 1, *far.shape[1:]), far.dtype),
+            jax.ShapeDtypeStruct(far.shape, far.dtype),
+            jax.ShapeDtypeStruct((2, *far.shape), far.dtype),
             jax.ShapeDtypeStruct(near.shape, near.dtype),
-            jax.ShapeDtypeStruct(far.shape[1:], far.dtype),
+            jax.ShapeDtypeStruct(far.shape, far.dtype),
+            jax.ShapeDtypeStruct((2, *near.shape), near.dtype),
+            jax.ShapeDtypeStruct((2, *far.shape), far.dtype),
         ),
-        in_specs=[WHOLE] * 3 + [ANY] * 2,
-        out_specs=[ANY] * 7,
+        in_specs=[WHOLE] * 3 + [ANY] * 4,
+        out_specs=[ANY] * 9,
         scratch_shapes=[
             dma((kinds,)), dma((kinds,)),
             dma((peers - 1, kinds)), dma((peers - 1, kinds)),
@@ -496,14 +520,14 @@
             dma((2,)), dma((2,)),
             dma((2, 4 * planes)), dma((2, 4 * planes)),
             dma((2, 4 * planes, 2)), dma((2, 4 * planes, 2)),
-            dma(far.shape[:2]), dma(far.shape[:2]),
+            dma((3, kinds)), dma((3, kinds)),
             dma((2 + kinds,)),
         ],
         compiler_params=pltpu.CompilerParams(
             collective_id=0, has_side_effects=True, vmem_limit_bytes=24 << 20
         ),
         name="spread",
-    )(weights, tokens, upstream, far, near)
+    )(weights, tokens, upstream, far, near, *others)
 
 
 def add_rows(target, left, right, step=256):
@@ -573,8 +597,8 @@
                 self.own(kind).wait()
 
 
-def swap_sum_kernel(peers, width, packed, partial, arrived, shares, send, recv, own_sem,
-                    from_core, both_cores, from_chip, c_send, c_recv, x_send, x_recv):
+def swap_sum_kernel(scale, peers, width, packed, hidden, down, arrived, shares, send, recv,
+                    own_sem, partial, from_core, both_cores, from_chip, c_send, c_recv, x_send, x_recv):
     unit = lax.axis_index("mp")
     core, chip = other_core(unit), other_chip(unit)
     grads = Grads(peers, width, packed, arrived, send, recv, own_sem)
@@ -590,10 +614,29 @@
             columns(whose), from_core.at[far], c_send.at[far], c_recv.at[far], mp=core
         )
 
+    def multiply(unit, step=256):
+        first = pl.multiple_of(unit * share, share)
+        features = down[pl.ds(first, share), :]
+
+        def some(number, carry):
+            here = pl.ds(pl.multiple_of(number * step, step), step)
+            value = lax.dot_general(
+                hidden[here, :], features, (((1,), (1,)), ((), ())),
+                preferred_element_type=jnp.float32,
+            )
+            partial[here, pl.ds(first, share)] = (value * scale).astype(partial.dtype)
+            return carry
+
+        lax.fori_loop(0, partial.shape[0] // step, some, 0)
+
     across = remote(both_cores, from_chip, x_send, x_recv, mp=chip)
-    for far in (1, 0):
-        to_core(far).start()
     grads.start()
+    multiply(other_chip(core))
+    multiply(core)
+    to_core(1).start()
+    multiply(chip)
+    to_core(0).start()
+    multiply(unit)
     to_core(1).wait_recv()
     add_rows(both_cores, columns(chip), from_core.at[1])
     to_core(0).wait_recv()
@@ -666,36 +709,38 @@
     grads.wait()
 
 
-def swap(kernel, packed, columns, kinds, other, gives, more, collective_id):
+def swap(kernel, packed, columns, kinds, others, gives, more, collective_id):
     peers, rows, across = packed.shape
     dma = pltpu.SemaphoreType.DMA
     return pl.pallas_call(
         functools.partial(kernel, peers, across // kinds),
         out_shape=[
             jax.ShapeDtypeStruct((kinds, rows, columns), packed.dtype),
-            jax.ShapeDtypeStruct(gives, other.dtype),
+            jax.ShapeDtypeStruct(gives, packed.dtype),
         ],
-        in_specs=[WHOLE] * 2,
+        in_specs=[WHOLE] * (1 + len(others)),
         out_specs=[ANY, WHOLE],
         scratch_shapes=[dma((peers - 1, kinds)), dma((peers - 1, kinds)), dma((kinds,)), *more],
         compiler_params=pltpu.CompilerParams(
             collective_id=collective_id, has_side_effects=True, vmem_limit_bytes=40 << 20
         ),
         name="swap",
-    )(packed, other)
-
-
-def swap_sum(packed, columns, kinds, partial):
-    rows, features = partial.shape
+    )(packed, *others)
+
+
+def swap_sum(packed, columns, kinds, hidden, down, scale):
+    rows, features = hidden.shape[0], down.shape[0]
     share = (rows, features // 4)
     dma = pltpu.SemaphoreType.DMA
     more = [
-        pltpu.VMEM((2, *share), partial.dtype),
-        pltpu.VMEM(share, partial.dtype),
-        pltpu.VMEM(share, partial.dtype),
+        pltpu.VMEM((rows, features), packed.dtype),
+        pltpu.VMEM((2, *share), packed.dtype),
+        pltpu.VMEM(share, packed.dtype),
+        pltpu.VMEM(share, packed.dtype),
         dma((2,)), dma((2,)), dma, dma,
     ]
-    return swap(swap_sum_kernel, packed, columns, kinds, partial, share, more, 1)
+    kernel = functools.partial(swap_sum_kernel, scale)
+    return swap(kernel, packed, columns, kinds, (hidden, down), share, more, 1)
 
 
 def swap_shares(packed, columns, kinds, shares):
@@ -705,7 +750,7 @@
     dma = pltpu.SemaphoreType.DMA
     more = [pltpu.VMEM(landed, shares.dtype)] * 2
     more += [dma((planes,)), dma((planes,)), dma((planes - 1,)), dma((planes - 1,)), dma]
-    return swap(swap_shares_kernel, packed, columns, kinds, shares, landed, more, 2)
+    return swap(swap_shares_kernel, packed, columns, kinds, (shares,), landed, more, 2)
 
 
 STEP_ROWS = 72
@@ -827,42 +872,33 @@
     )(numbers, *states, *(value for pair in moved for value in pair), grads, last_grads)
 
 
-def cast_kernel(*refs):
-    owns, near, near_rest, far, weights = refs[:3], *refs[3:]
+def cast_kernel(own, near, far, weights):
     half = near.shape[1]
-    for which in range(3):
-        target = near_rest.at[which - 1, 0] if which else near.at[0]
-        target[...] = owns[which][0, :half, :].astype(near.dtype)
-        far[which, 0] = owns[which][0, half:, :].astype(far.dtype)
-    weights[0] = owns[0][0].astype(weights.dtype)
-
-
-def cast(states):
-    kinds, rows, columns = states[0].shape
+    near[0] = own[0, :half, :].astype(near.dtype)
+    far[0] = own[0, half:, :].astype(far.dtype)
+    weights[0] = own[0].astype(weights.dtype)
+
+
+def cast(state):
+    kinds, rows, columns = state.shape
     width = columns // 2 if columns % 256 == 0 else columns
     half = (rows + 15) // 16 * 8
-
-    def one(rows):
-        return pl.BlockSpec((1, rows, width), lambda kind, part: (kind, 0, part))
-
-    def several(count, rows):
-        return pl.BlockSpec((count, 1, rows, width), lambda kind, part: (0, kind, 0, part))
-
-    shapes = [
-        (kinds, half, columns),
-        (2, kinds, half, columns),
-        (3, kinds, rows - half, columns),
-        (kinds, rows, columns),
-    ]
+    counts = (half, rows - half, rows)
+
+    def block(count):
+        return pl.BlockSpec((1, count, width), lambda kind, part: (kind, 0, part))
+
     return pl.pallas_call(
         cast_kernel,
-        out_shape=[jax.ShapeDtypeStruct(shape, jnp.bfloat16) for shape in shapes],
+        out_shape=[
+            jax.ShapeDtypeStruct((kinds, count, columns), jnp.bfloat16) for count in counts
+        ],
         grid=(kinds, columns // width),
-        in_specs=[one(rows)] * 3,
-        out_specs=[one(half), several(2, half), several(3, rows - half), one(rows)],
+        in_specs=[block(rows)],
+        out_specs=[block(count) for count in counts],
         compiler_params=pltpu.CompilerParams(vmem_limit_bytes=32 << 20),
         name="cast",
-    )(*states)
+    )(state)
 
 
 def unpack_kernel(numbers, block, *refs):
@@ -968,9 +1004,10 @@
     )
 
 
-def token_pass(tokens, upstream, weights, far, near, old_offsets, new_offsets, capacity_new):
+def token_pass(tokens, upstream, casts, others, old_offsets, new_offsets, capacity_new):
     peers = lax.axis_size("dp")
     feature_peers = lax.axis_size("mp")
+    near, far, weights = casts
     kinds, _, columns = weights.shape
     width = lane_split(columns, peers)
     features = tokens.shape[1]
@@ -979,7 +1016,7 @@
     busy = lax.axis_index("dp") != IDLE
 
     blocks, all_tokens, all_upstream, *arrived = spread(
-        weights, tokens, upstream, far, near, peers, width
+        weights, tokens, upstream, far, near, others, peers, width
     )
     rows = unpack(blocks, old_offsets, busy, features, kinds)
 
@@ -994,8 +1031,6 @@
     up_grad = (back_grad * gate_act * sigmoid_gate).astype(jnp.bfloat16)
     gate_grad, up_grad = lax.optimization_barrier((gate_grad, up_grad))
 
-    partial_value = (product(hidden, rows[2], 1, 1) * scale_hidden).astype(jnp.bfloat16)
-
     grads = [
         (product(all_tokens, gate_grad, 0, 0) * scale_in).astype(jnp.bfloat16),
         (product(all_tokens, up_grad, 0, 0) * scale_in).astype(jnp.bfloat16),
@@ -1003,7 +1038,7 @@
     last_grads = (product(all_upstream, hidden, 0, 0) * scale_hidden).astype(jnp.bfloat16)
     first_packed = pack(grads, new_offsets, capacity_new)
     last_packed = pack([last_grads], new_offsets, capacity_new)
-    grads, shares = swap_sum(first_packed, columns, kinds - 1, partial_value)
+    grads, shares = swap_sum(first_packed, columns, kinds - 1, hidden, rows[2], scale_hidden)
     last_grads, shares = swap_shares(last_packed, columns, 1, shares)
     layer_output = jnp.sum(shares.astype(jnp.float32), axis=0).astype(jnp.bfloat16)
     return grads, last_grads, layer_output, arrived
@@ -1026,12 +1061,13 @@
     upstream = jnp.where(live_flag, out_grad, jnp.zeros_like(out_grad))
 
     states = [value.transpose(1, 0, 2) for value in (master, moment_one, moment_two)]
-    near, near_rest, far, weights = cast(states)
+    casts = cast(states[0])
+    near = casts[0]
+    grads, last_grads, layer_output, landed = token_pass(
+        tokens, upstream, casts, states[1:], old_offsets, new_offsets, capacity_new
+    )
+    straight, straight_rest, hopped, relayed, near_rest, _ = landed
     near_rest = lax.ppermute(near_rest, "dp", [(i, i + 1) for i in range(devices - 1)])
-    grads, last_grads, layer_output, landed = token_pass(
-        tokens, upstream, weights, far, near, old_offsets, new_offsets, capacity_new
-    )
-    straight, straight_rest, hopped, relayed = landed
     pairs = [(i, i + 1 - 2 * (i % 2)) for i in range(devices) if i != 1]
     near = lax.ppermute(jnp.where(device_index % 2 > 0, hopped, near), "dp", pairs)
     pairs = [(i, i + 2) for i in range(0, devices - 2, 2)]

time: 486 us -> 427 us (0.88)
  Pallas kernels: 397 us -> 345 us
  matrix products: 33.7 us -> 28 us
  starting transfers between devices: 24.5 us -> 19.4 us
    pallas_call x1, Pallas kernels: 219 us -> 162 us  [spread(): pl.pallas_call(functools.partial(spread_kernel, peers, width), out_shape=...]
    pallas_call x2, Pallas kernels: 134 us -> 145 us  [swap(): pl.pallas_call(functools.partial(kernel, peers, across // kinds), out_sha...]
    pallas_call x1, Pallas kernels: 7.83 us -> 1.74 us  [cast(): pl.pallas_call(cast_kernel, out_shape=[jax.ShapeDtypeStruct((kinds, count...]
    dot_general x7 -> x6, matrix products: 33.7 us -> 28 us  [product(): lax.dot_general(left, right, (((left_dim,), (right_dim,)), ((), ())), pre...]
    unnamed x42 -> x48, local copies, waits for them, and re-layouts: 18.6 us -> 19.2 us
  transfers between devices with their start and end apart: 3 -> 3, of which waited for: 0 -> 0; matrix products, arithmetic and copies ran while one was open for 8% -> 7% of each run, Pallas kernels for 75% -> 37%
where the time goes in v3:
time: 427 us; the launch traced here: 422 us
  Pallas kernels  345 us (81%)
  matrix products  28 us (7%)
  starting transfers between devices  19.4 us (5%)
  local copies, waits for them, and re-layouts  19.2 us (4%)
  between operations  5.89 us (1%)
  other arithmetic  4.6 us (1%)
    pallas_call x1, Pallas kernels, spread(): pl.pallas_call(functools.partial(spread_kernel, peers, width), out_shape=...  162 us
    pallas_call x2, Pallas kernels, swap(): pl.pallas_call(functools.partial(kernel, peers, across // kinds), out_sha...  145 us
    dot_general x6, matrix products, product(): lax.dot_general(left, right, (((left_dim,), (right_dim,)), ((), ())), pre...  28 us
    pallas_call x1, Pallas kernels, adam(): pl.pallas_call(adam_kernel, out_shape=[jax.ShapeDtypeStruct((kinds, capac...  25.2 us
    unnamed x48, local copies, waits for them, and re-layouts  19.2 us
    ppermute x1, starting transfers between devices, token_step(): relayed_rest = lax.ppermute(straight_rest, 'dp', pairs)  13.3 us
  transfers between devices with their start and end apart: 3, of which 0 were waited for; matrix products, arithmetic and copies ran while one was open for 7% of the time, Pallas kernels for 37%

profile of v3, /device:TPU:9, one launch (start us, length us, event | category | flops | bytes accessed | tf_op | source)
XLA Modules:
  0.0 422.2 jit_solution(10495105739286207900)
XLA Ops:
  0.7 2.8 copy-done
  3.5 1.7 cast.1
  5.2 1.7 copy-done.3
  10.0 1.9 copy-done.4
  11.9 162.1 %spread.1 = (bf16[8,296,768]{2,1,0:T(8,128)(2,1)S(1)}, bf16[2048,2048]{1,0:T(8,128)(2,1)}, bf16[2048,2048]{1,0:T(8,128)(2,1)}, bf16[3,144,1792]{2,1,0:T(8,128)(2...) custom-call(bf16[3,296,1792]{2,1,0:T(8,128)(2,1)S(1)} %copy-done.4, ...), custom_call_target="tpu_custom_call" | custom-call | tf_op jit(solution)/shard_map/spread/pallas_call | solution.py:501
  176.3 1.5 broadcast_select_fusion
  178.6 4.0 collective-permute-start
  182.6 13.3 %collective-permute-start.2 = (bf16[2,3,144,1792]{3,2,1,0:T(8,128)(2,1)}, bf16[2,3,144,1792]{3,2,1,0:T(8,128)(2,1)}, u32[]{:S(2)}, u32[]{:S(2)}) collective-permute-start(bf16[2,3,144,1792]{3,2,1,0:T(8,128)(2,1)} %get-tuple-element.33.refs_6_), channel_id=1, source_target_pairs={{0,8},{8,16},{16,24},{1,9},{9,17},{17,25},{2,10},{10,18},{18,26},{... | collective-permute-start | bytes 9289736 | tf_op jit(solution)/shard_map/ppermute | solution.py:1074
  196.0 2.1 collective-permute-start.1
  198.2 2.0 copy-done.2
  200.2 4.6 %unpack.1 = (bf16[2048,256]{1,0:T(8,128)(2,1)S(1)}, bf16[2048,256]{1,0:T(8,128)(2,1)S(1)}, bf16[2048,256]{1,0:T(8,128)(2,1)S(1)}) custom-call(s32[10]{0:T(128)S(1)} %pad_add_fusion.1.numbers, bf16[8,296,768]{2,1,0:T(8,128)(2,1)S(1)} %copy-done.2), custom_call_target="tpu_custom_call" | custom-call | tf_op jit(solution)/shard_map/unpack/pallas_call | solution.py:939
  204.8 6.0 %convolution_multiply_fusion.3 = f32[2048,256]{1,0:T(8,128)S(1)} fusion(bf16[2048,2048]{1,0:T(8,128)(2,1)} %get-tuple-element.35, bf16[2048,256]{1,0:T(8,128)(2,1)S(1)} %get-tuple-element.40), kind=kOutput, calls=%fused_computation.3 | convolution fusion | flops 2148007936 | bytes 11534336 | tf_op jit(solution)/shard_map/dot_general | solution.py:999
  210.9 2.4 convolution_multiply_fusion.5
  213.3 4.9 %multiply_convert_fusion = (bf16[2048,256]{1,0:T(8,128)(2,1)S(1)}, bf16[2048,256]{1,0:T(8,128)(2,1)}, bf16[2048,256]{1,0:T(8,128)(2,1)}) fusion(f32[2048,256]{1,0:T(8,128)S(1)} %convolution_multiply_fusion.3, f32[2048,256]{1,0:T(8,128)S(1)} %convolution_multiply_fusion.5, bf16[2048,2048]{1,0:T(8,128)(2,1)S(1)} %bitcast.30, ...), kind=kOutput, calls=%fused_computation.9 | convolution fusion | flops 2156396544 | bytes 16777216 | tf_op jit(solution)/shard_map/dot_general | solution.py:999
  222.6 6.0 %fusion.2.refs_0_ = bf16[2048,256]{1,0:T(8,128)(2,1)S(1)} fusion(bf16[2048,2048]{1,0:T(8,128)(2,1)} %get-tuple-element.36, bf16[2048,256]{1,0:T(8,128)(2,1)S(1)} %get-tuple-element.54.hidden), kind=kOutput, calls=%fused_computation.8 | convolution fusion | flops 2148532224 | bytes 10485760 | tf_op jit(solution)/shard_map/dot_general | solution.py:999
  229.6 2.9 pack.3.packed
  232.6 6.1 %fusion.refs_0_ = bf16[2048,256]{1,0:T(8,128)(2,1)S(1)} fusion(bf16[2048,2048]{1,0:T(8,128)(2,1)} %get-tuple-element.35, bf16[2048,256]{1,0:T(8,128)(2,1)S(1)} %copy-done.17), kind=kOutput, calls=%fused_computation.6 | convolution fusion | flops 2148532224 | bytes 10485760 | tf_op jit(solution)/shard_map/dot_general | solution.py:999
  238.7 2.6 fusion.1.refs_1_
  241.3 3.6 pack.2.packed
  244.9 78.1 %swap.2 = (bf16[2,360,1792]{2,1,0:T(8,128)(2,1)S(1)}, bf16[2048,512]{1,0:T(8,128)(2,1)S(1)}) custom-call(bf16[8,360,512]{2,1,0:T(8,128)(2,1)S(1)} %pack.2.packed, bf16[2048,256]{1,0:T(8,128)(2,1)S(1)} %copy-done.13, bf16[2048,256]{1,0:T(8,128)(2,1)S(1)} %get-tuple-element.38.down), custom_call_target="tpu_custom_call" | custom-call | tf_op jit(solution)/shard_map/swap/pallas_call | solution.py:715
  323.0 1.5 copy-done.5
  325.8 1.6 copy-done.7
  327.4 67.0 %swap.3 = (bf16[1,360,1792]{2,1,0:T(8,128)(2,1)S(1)}, bf16[4,256,512]{2,1,0:T(8,128)(2,1)S(1)}) custom-call(bf16[8,360,256]{2,1,0:T(8,128)(2,1)S(1)} %pack.3.packed, bf16[2048,512]{1,0:T(8,128)(2,1)S(1)} %copy-done.7), custom_call_target="tpu_custom_call" | custom-call | tf_op jit(solution)/shard_map/swap/pallas_call | solution.py:715
  397.0 25.2 %adam.1 = (f32[3,360,1792]{2,1,0:T(8,128)}, f32[3,360,1792]{2,1,0:T(8,128)}, f32[3,360,1792]{2,1,0:T(8,128)}) custom-call(s32[4]{0:T(128)} %pad_add_fusion.numbers, f32[3,296,1792]{2,1,0:T(8,128)} %bitcast.23, f32[3,296,1792]{2,1,0:T(8,128)} %bitcast.26, f32[3,296,1792]{2,1,0:T(8,128)} %bitcast.28, bf16[3,152,1792]{2,1,0:T(8,128)(2,1)} %collective-permute-done.refs_3_, ...), custom_call_target="tpu_custom_call" | custom-call | tf_op jit(solution)/shard_map/adam/pallas_call | solution.py:855
  (55 shorter events, 10.9 us)
Async XLA Ops:
  0.6 2.8 copy-start
  3.5 3.4 copy-start.14
  5.2 1.7 copy-start.3
  8.7 1.2 copy-start.11
  10.0 1.9 copy-start.4
  174.0 1.2 copy-start.8
  176.3 2.4 copy-start.1
  176.3 21.8 %copy-start.15 = (s32[9]{0:T(128)S(1)}, s32[9]{0:T(128)}, u32[]{:S(2)}) copy-start(s32[9]{0:T(128)} %param.12) | copy-start | bytes 112
  178.6 218.3 %collective-permute-start = (bf16[3,152,1792]{2,1,0:T(8,128)(2,1)}, bf16[3,152,1792]{2,1,0:T(8,128)(2,1)}, u32[]{:S(2)}, u32[]{:S(2)}) collective-permute-start(bf16[3,152,1792]{2,1,0:T(8,128)(2,1)} %broadcast_select_fusion), channel_id=1, source_target_pairs={{0,4},{8,12},{12,8},{16,20},{20,16},{24,28},{28,24},{1,5},{9,13},{... | collective-permute-start | bytes 4902920 | tf_op jit(solution)/shard_map/ppermute | solution.py:1072
  182.6 214.3 %collective-permute-start.2 = (bf16[2,3,144,1792]{3,2,1,0:T(8,128)(2,1)}, bf16[2,3,144,1792]{3,2,1,0:T(8,128)(2,1)}, u32[]{:S(2)}, u32[]{:S(2)}) collective-permute-start(bf16[2,3,144,1792]{3,2,1,0:T(8,128)(2,1)} %get-tuple-element.33.refs_6_), channel_id=1, source_target_pairs={{0,8},{8,16},{16,24},{1,9},{9,17},{17,25},{2,10},{10,18},{18,26},{... | collective-permute-start | bytes 9289736 | tf_op jit(solution)/shard_map/ppermute | solution.py:1074
  196.0 201.0 %collective-permute-start.1 = (bf16[2,3,152,1792]{3,2,1,0:T(8,128)(2,1)}, bf16[2,3,152,1792]{3,2,1,0:T(8,128)(2,1)}, u32[]{:S(2)}, u32[]{:S(2)}) collective-permute-start(bf16[2,3,152,1792]{3,2,1,0:T(8,128)(2,1)} %get-tuple-element.31), channel_id=1, source_target_pairs={{0,4},{4,8},{8,12},{12,16},{16,20},{20,24},{24,28},{1,5},{5,9},{9,... | collective-permute-start | bytes 9805832 | tf_op jit(solution)/shard_map/ppermute | solution.py:1070
  198.2 2.0 copy-start.2
  200.2 10.6 %slice-start.4 = ((s8[8388608]{0:T(1024)(128)(4,1)}), s8[4194304]{0:T(1024)(128)(4,1)S(1)}, s32[]{:S(2)}) async-start(s8[8388608]{0:T(1024)(128)(4,1)} %bitcast.33), calls=%async_computation.4 | async-start | bytes 8388608
  204.8 6.0 %slice-start.5 = ((s8[8388608]{0:T(1024)(128)(4,1)}), s8[4194304]{0:T(1024)(128)(4,1)S(1)}, s32[]{:S(2)}) async-start(s8[8388608]{0:T(1024)(128)(4,1)} %bitcast.33), calls=%async_computation.5 | async-start | bytes 8388608
  204.8 8.5 %slice-start = ((s8[8388608]{0:T(1024)(128)(4,1)}), s8[4194304]{0:T(1024)(128)(4,1)S(1)}, s32[]{:S(2)}) async-start(s8[8388608]{0:T(1024)(128)(4,1)} %bitcast.29), calls=%async_computation | async-start | bytes 8388608
  210.8 2.5 slice-start.1
  222.6 10.0 %copy-start.17 = (bf16[2048,256]{1,0:T(8,128)(2,1)S(1)}, bf16[2048,256]{1,0:T(8,128)(2,1)}, u32[]{:S(2)}) copy-start(bf16[2048,256]{1,0:T(8,128)(2,1)} %get-tuple-element.41) | copy-start | bytes 3145732
  229.6 9.0 %slice-start.2 = ((s8[8388608]{0:T(1024)(128)(4,1)}), s8[4194304]{0:T(1024)(128)(4,1)S(1)}, s32[]{:S(2)}) async-start(s8[8388608]{0:T(1024)(128)(4,1)} %bitcast.31), calls=%async_computation.2 | async-start | bytes 8388608
  232.6 6.1 %slice-start.3 = ((s8[8388608]{0:T(1024)(128)(4,1)}), s8[4194304]{0:T(1024)(128)(4,1)S(1)}, s32[]{:S(2)}) async-start(s8[8388608]{0:T(1024)(128)(4,1)} %bitcast.31), calls=%async_computation.3 | async-start | bytes 8388608
  232.6 6.1 %copy-start.16 = (bf16[2048,256]{1,0:T(8,128)(2,1)S(1)}, bf16[2048,256]{1,0:T(8,128)(2,1)}, u32[]{:S(2)}) copy-start(bf16[2048,256]{1,0:T(8,128)(2,1)} %get-tuple-element.42) | copy-start | bytes 3145732
  241.3 3.6 copy-start.13
  323.0 1.5 copy-start.5
  324.5 1.3 copy-start.6
  325.8 1.6 copy-start.7
  (3 other events, 3.3 us)
